TPU v7x, 256 devices: a whole 4x4x8 slice. The times are simulated.
256 devices in a mesh: lat: 8 (over z_lo, core), lon: 8 (over z_hi, x), chan: 4 (over y).
Axes of the slice: x: 4, y: 4, z: 8 (z_hi: 2, z_lo: 4; z = z_hi * 4 + z_lo), core: 2. Of those that a mesh axis runs over, the one named last changes fastest.
Arguments:
- queries: bfloat16 [128, 64, 2560], P('lat', 'lon', 'chan'), may hold values from -8 to 8
- keys: bfloat16 [128, 64, 2560], P('lat', 'lon', 'chan'), may hold values from -8 to 8
- values: bfloat16 [128, 64, 2560], P('lat', 'lon', 'chan'), may hold values from -6 to 6
- attn_out: bfloat16 [128, 64, 2560], P('lat', 'lon', 'chan'), may hold values from -6 to 6
- grad_out: bfloat16 [128, 64, 5120], P('lat', 'lon', 'chan'), may hold values from -6 to 6
- w_out: bfloat16 [5120, 2560], P(('lat', 'lon'), 'chan'), may hold values from -0.078125 to 0.078125
- bias_table: float32 [20, 25, 13], P('chan'), may hold values from -5 to 5
- key_mask: int32 [128, 64], replicated, may hold values 0 or 1
Outputs:
- grad_queries: bfloat16 [128, 64, 2560], P('lat', 'lon', 'chan')
- grad_keys: bfloat16 [128, 64, 2560], P('lat', 'lon', 'chan')
- grad_values: bfloat16 [128, 64, 2560], P('lat', 'lon', 'chan')
- grad_wout: float32 [5120, 2560], P(('lat', 'lon'), 'chan')
- grad_table: float32 [20, 25, 13], P('chan')
All inputs are finite; a program needn't handle non-finite values.
Results may differ from a plain program's by a relative error of at most 0.007.
Values may be sent and summed in bfloat16 or wider, within the bound.
No kernel may reach another device: no remote copies, remote signals or barrier semaphores. Data moves between devices by JAX's collectives and lax.ppermute only.
A program may use at most 128 MiB of HBM per device.

v0:
```python
import jax
import jax.numpy as jnp
from jax import lax
from jax.sharding import PartitionSpec as P

HEAD_DIM = 128
WIN = 13


def extended_2(value, sides, width, wrap):
    for axis, dim in sides:
        count, length = (lax.axis_size(axis), value.shape[dim])
        up = [(i, (i + 1) % count) for i in range(count if wrap else count - 1)]
        down = [(j, i) for i, j in up]
        last = lax.slice_in_dim(value, length - width, length, axis=dim)
        leading = lax.slice_in_dim(value, 0, width, axis=dim)
        before = lax.ppermute(last, axis, up)
        after = lax.ppermute(leading, axis, down)
        value = jnp.concatenate([before, value, after], axis=dim)
    return value


def fold_lon(extended, core_width):
    full_width = extended.shape[2]
    reach_cells = (full_width - core_width) // 2
    rim_cells = jnp.concatenate(
        [extended[:, :, :reach_cells], extended[:, :, full_width - reach_cells :]], axis=2
    )
    received = extended_2(rim_cells.astype(jnp.bfloat16), (("lon", 2),), reach_cells, True).astype(
        rim_cells.dtype
    )
    middle = extended[:, :, reach_cells : full_width - reach_cells]
    front_add = jnp.pad(
        received[:, :, :reach_cells], ((0, 0), (0, 0), (0, core_width - reach_cells), (0, 0))
    )
    back_add = jnp.pad(
        received[:, :, 3 * reach_cells :], ((0, 0), (0, 0), (core_width - reach_cells, 0), (0, 0))
    )
    return middle + front_add + back_add


def fold_lat(extended, core_width):
    full_width = extended.shape[1]
    reach_cells = (full_width - core_width) // 2
    rim_cells = jnp.concatenate(
        [extended[:, :reach_cells], extended[:, full_width - reach_cells :]], axis=1
    )
    received = extended_2(rim_cells.astype(jnp.bfloat16), (("lat", 1),), reach_cells, False).astype(
        rim_cells.dtype
    )
    middle = extended[:, reach_cells : full_width - reach_cells]
    front_add = jnp.pad(
        received[:, :reach_cells], ((0, 0), (0, core_width - reach_cells), (0, 0), (0, 0))
    )
    back_add = jnp.pad(
        received[:, 3 * reach_cells :], ((0, 0), (core_width - reach_cells, 0), (0, 0), (0, 0))
    )
    return middle + front_add + back_add


def local(queries, keys, values, attn_out, grad_out, w_out, bias_table, key_mask):
    lat_rows, lon_cols, chan_width = queries.shape
    head_count = bias_table.shape[0]
    reach_cells = WIN // 2
    score_scale = HEAD_DIM ** (-0.5)
    tokens = lat_rows * lon_cols
    ext_rows = lat_rows + 2 * reach_cells
    ext_cols = lon_cols + 2 * reach_cells
    row_block = 4
    key_span = row_block + WIN - 1
    block_count = lat_rows // row_block
    block_rows = row_block * lon_cols
    block_keys = key_span * ext_cols
    offset_rows = 2 * WIN - 1
    low_pad = row_block - 1
    lat_total = lat_rows * lax.axis_size("lat")
    lon_total = lon_cols * lax.axis_size("lon")
    contract_lead = (((0,), (0,)), ((), ()))
    full_grad = lax.all_gather(grad_out, "chan", axis=2, tiled=True).reshape(tokens, -1)
    grad_cols = jnp.transpose(full_grad)
    slab_part = grad_cols
    grad_attn = lax.dot_general(
        slab_part,
        lax.all_gather(w_out, ("lat", "lon"), axis=0, tiled=True),
        contract_lead,
        preferred_element_type=jnp.float32,
    ).astype(jnp.bfloat16)
    kv_pair = jnp.stack([keys, values])
    extended = extended_2(kv_pair, (("lat", 1), ("lon", 2)), reach_cells, True)
    lat_first = lax.axis_index("lat") * lat_rows
    lon_first = lax.axis_index("lon") * lon_cols
    ext_col = lon_first - reach_cells + jnp.arange(ext_cols, dtype=jnp.int32)
    wrap_col = ext_col % lon_total
    mask_cols = jnp.take(key_mask, wrap_col, axis=1)
    mark_cols = wrap_col % 4 == 0
    rel_lon = (
        jnp.arange(ext_cols, dtype=jnp.int32)[None, :]
        - jnp.arange(lon_cols, dtype=jnp.int32)[:, None]
    )
    in_lon = (rel_lon >= 0) & (rel_lon < WIN)
    lon_pick = jnp.clip(rel_lon, 0, WIN - 1)
    lon_table = jnp.take(bias_table, lon_pick, axis=2).transpose(0, 2, 1, 3)
    table_pad = jnp.pad(lon_table, ((0, 0), (0, 0), (low_pad, low_pad), (0, 0)))
    query_heads = queries.reshape(lat_rows, lon_cols, head_count, HEAD_DIM)
    grad_heads = grad_attn.reshape(lat_rows, lon_cols, head_count, HEAD_DIM)

    def block_step(state_pair, block_index):
        grad_pair, table_acc = state_pair
        local_first = block_index * row_block
        top_row = lat_first + local_first
        key_first = jnp.clip(top_row - reach_cells, 0, lat_total - key_span)
        key_local = key_first - (lat_first - reach_cells)
        query_rows = top_row + jnp.arange(row_block, dtype=jnp.int32)
        window_first = jnp.clip(query_rows - reach_cells, 0, lat_total - WIN)
        key_glob = key_first + jnp.arange(key_span, dtype=jnp.int32)
        in_lat = (key_glob[None, :] >= window_first[:, None]) & (
            key_glob[None, :] < window_first[:, None] + WIN
        )
        mask_rows = lax.dynamic_slice_in_dim(mask_cols, key_first, key_span, 0)
        valid_keys = (mask_rows == 1) | (key_glob % 4 == 0)[:, None] & mark_cols[None, :]
        allowed = in_lat[:, None, :, None] & in_lon[None, :, None, :] & valid_keys[None, None, :, :]
        allowed = allowed.reshape(block_rows, block_keys)
        shifts = key_first - query_rows + (WIN - 1) + low_pad
        bias_parts = [
            lax.dynamic_slice_in_dim(table_pad, shifts[row_pos], key_span, 2)
            for row_pos in range(row_block)
        ]
        bias_rows = jnp.stack(bias_parts, axis=1).reshape(head_count, block_rows, block_keys)
        query_block = lax.dynamic_slice_in_dim(query_heads, local_first, row_block, 0).reshape(
            block_rows, head_count, HEAD_DIM
        )
        grad_block = lax.dynamic_slice_in_dim(grad_heads, local_first, row_block, 0).reshape(
            block_rows, head_count, HEAD_DIM
        )
        pair_block = lax.dynamic_slice_in_dim(extended, key_local, key_span, 1).reshape(
            2, block_keys, head_count, HEAD_DIM
        )
        key_block = pair_block[0]
        value_block = pair_block[1]
        scores = (
            score_scale
            * jnp.einsum("qhd,khd->hqk", query_block, key_block, preferred_element_type=jnp.float32)
            + bias_rows
        )
        scores = jnp.where(allowed[None], scores, -1e30)
        row_max = jnp.max(scores, axis=2, keepdims=True)
        weights_exp = jnp.exp(scores - row_max)
        prob_rows = weights_exp / jnp.sum(weights_exp, axis=2, keepdims=True)
        grad_prob = jnp.einsum(
            "qhd,khd->hqk", grad_block, value_block, preferred_element_type=jnp.float32
        )
        row_delta = jnp.sum(prob_rows * grad_prob, axis=2, keepdims=True)
        dscore = prob_rows * (grad_prob - row_delta)
        score_grid = dscore.reshape(head_count, row_block, lon_cols, key_span, ext_cols)
        score_grid = score_grid.transpose(0, 1, 3, 2, 4).reshape(
            head_count, row_block, key_span, lon_cols * ext_cols
        )
        for row_pos in range(row_block):
            prior_sum = lax.dynamic_slice_in_dim(table_acc, shifts[row_pos], key_span, 1)
            table_acc = lax.dynamic_update_slice_in_dim(
                table_acc, prior_sum + score_grid[:, row_pos], shifts[row_pos], 1
            )
        dscore_low = dscore.astype(jnp.bfloat16)
        prob_low = prob_rows.astype(jnp.bfloat16)
        grad_query = (
            score_scale
            * jnp.einsum("hqk,khd->qhd", dscore_low, key_block, preferred_element_type=jnp.float32)
        ).astype(jnp.bfloat16)
        key_part = score_scale * jnp.einsum(
            "hqk,qhd->khd", dscore_low, query_block, preferred_element_type=jnp.float32
        )
        value_part = jnp.einsum(
            "hqk,qhd->khd", prob_low, grad_block, preferred_element_type=jnp.float32
        )
        new_part = jnp.stack([key_part, value_part]).reshape(2, key_span, ext_cols, chan_width)
        prior_pair = lax.dynamic_slice_in_dim(grad_pair, key_local, key_span, 1)
        grad_pair = lax.dynamic_update_slice_in_dim(grad_pair, prior_pair + new_part, key_local, 1)
        return ((grad_pair, table_acc), grad_query)

    zero_pair = jnp.zeros((2, ext_rows, ext_cols, chan_width), jnp.float32)
    zero_table = jnp.zeros(
        (head_count, offset_rows + 2 * low_pad, lon_cols * ext_cols), jnp.float32
    )
    (grad_pair, table_acc), query_blocks = lax.scan(
        block_step, (zero_pair, zero_table), jnp.arange(block_count, dtype=jnp.int32)
    )
    grad_queries = query_blocks.reshape(lat_rows, lon_cols, chan_width)
    table_core = table_acc[:, low_pad : low_pad + offset_rows].reshape(
        head_count, offset_rows, lon_cols, ext_cols
    )
    col_take = (
        jnp.arange(lon_cols, dtype=jnp.int32)[:, None] + jnp.arange(WIN, dtype=jnp.int32)[None, :]
    )
    col_take = jnp.broadcast_to(
        col_take[None, None, :, :], (head_count, offset_rows, lon_cols, WIN)
    )
    table_local = jnp.sum(jnp.take_along_axis(table_core, col_take, axis=3), axis=2)
    grad_table = lax.psum(table_local, ("lat", "lon"))
    folded = fold_lat(fold_lon(grad_pair, lon_cols), lat_rows)
    grad_keys = folded[0].astype(jnp.bfloat16)
    grad_values = folded[1].astype(jnp.bfloat16)
    saved_out = attn_out.reshape(tokens, chan_width)
    slab_part = grad_cols
    grad_wout = lax.psum_scatter(
        jnp.dot(slab_part, saved_out, preferred_element_type=jnp.float32),
        ("lat", "lon"),
        scatter_dimension=0,
        tiled=True,
    )
    return (grad_queries, grad_keys, grad_values, grad_wout, grad_table)


def solution(mesh):
    return jax.shard_map(
        local,
        mesh=mesh,
        in_specs=(
            P("lat", "lon", "chan"),
            P("lat", "lon", "chan"),
            P("lat", "lon", "chan"),
            P("lat", "lon", "chan"),
            P("lat", "lon", "chan"),
            P(("lat", "lon"), "chan"),
            P("chan", None, None),
            P(),
        ),
        out_specs=(
            P("lat", "lon", "chan"),
            P("lat", "lon", "chan"),
            P("lat", "lon", "chan"),
            P(("lat", "lon"), "chan"),
            P("chan", None, None),
        ),
        check_vma=False,
    )
```

profile of v0, /device:TPU:240, one launch (start us, length us, event | category | flops | bytes accessed | tf_op | source)
XLA Modules:
  0.0 933.4 jit_solution(14924076082434811027)
XLA Ops:
  9.8 26.9 %all-gather.3.cloned.1.call-done = bf16[16,8,5120]{2,0,1:T(8,128)(2,1)} async-done(((bf16[16,8,1280]{2,0,1:T(8,128)(2,1)}), bf16[16,8,5120]{2,0,1:T(8,128)(2,1)}) %all-gather.3.cloned.1.call-update) | async-done | bytes 1310736 | tf_op jit(solution)/shard_map/all_gather | solution.py:79
  36.7 7.9 convolution_bitcast_fusion.1
  51.5 4.6 collective-permute-start.3
  59.1 11.4 %collective-permute-done.3 = bf16[2,28,6,640]{3,0,2,1:T(2,128)(2,1)S(1)} collective-permute-done((bf16[2,28,6,640]{3,0,2,1:T(2,128)(2,1)S(1)}, bf16[2,28,6,640]{3,0,2,1:T(2,128)(2,1)S(1)}, u32[]{:S(2)}, u32[]{:S(2)}) %collective-permute-start.3) | collective-permute-done | bytes 430112 | tf_op jit(solution)/shard_map/ppermute | solution.py:18
  70.6 10.3 %collective-permute-done.2 = bf16[2,28,6,640]{3,0,2,1:T(2,128)(2,1)S(1)} collective-permute-done((bf16[2,28,6,640]{3,0,2,1:T(2,128)(2,1)S(1)}, bf16[2,28,6,640]{3,0,2,1:T(2,128)(2,1)S(1)}, u32[]{:S(2)}, u32[]{:S(2)}) %collective-permute-start.2) | collective-permute-done | bytes 430112 | tf_op jit(solution)/shard_map/ppermute | solution.py:17
  80.9 2.1 pad_maximum_fusion.1
  83.0 156.4 %all-gather.5.cloned.1.call-done = bf16[5120,640]{1,0:T(8,128)(2,1)} async-done(((bf16[80,640]{1,0:T(8,128)(2,1)}), bf16[5120,640]{1,0:T(8,128)(2,1)}) %all-gather.5.cloned.1.call-update) | async-done | bytes 6553616 | tf_op jit(solution)/shard_map/all_gather | solution.py:84
  239.4 4.6 fusion.42
  244.0 1.9 broadcast_in_dim.94
  245.9 117.0 %while.18 = (s32[]{:T(128)}, f32[2,28,20,640]{3,2,1,0:T(8,128)}, f32[5,31,160]{2,1,0:T(8,128)S(1)}, bf16[4,32,5,128]{3,1,2,0:T(8,128)(2,1)}, s32[4]{0:T(128)S(1)...) while((s32[]{:T(128)}, f32[2,28,20,640]{3,2,1,0:T(8,128)}, ...), condition=%wide.region_4.5_spmd.clone, body=%wide.region_0.0_spmd.clone.sunk | while | flops 67648624 | bytes 32509632 | solution.py:184
  259.8 1.9 dynamic-slice_bitcast_fusion.5
  272.1 3.0 fusion.106
  289.0 1.9 dynamic-slice_bitcast_fusion.5
  301.4 3.0 fusion.106
  330.6 3.1 fusion.106
  347.5 1.9 dynamic-slice_bitcast_fusion.5
  359.8 3.1 fusion.106
  363.0 2.2 convert.16
  367.6 2.0 collective-permute-start.4
  371.3 155.3 %gather_fusion.2 = f32[13000]{0:T(1024)S(1)} fusion(f32[5,25,8,20]{3,2,1,0:T(8,128)S(1)} %reshape.333, s32[13000]{0:T(1024)S(1)} %reshape.350), kind=kCustom, calls=%fused_computation.2 | custom fusion | bytes 312000 | tf_op jit(solution)/shard_map/jit(take_along_axis)/gather | solution.py:197
  529.9 2.3 fusion.59
  532.3 2.1 collective-permute-start.6
  534.3 4.4 collective-permute-start.7
  539.0 386.1 %psum.7 = f32[5,25,13]{2,1,0:T(8,128)S(1)} all-reduce(f32[5,25,13]{2,1,0:T(8,128)S(1)} %select_reduce_fusion), channel_id=1, replica_groups=mesh['lat'=8,'lon'=8,'chan'=4] {'lat','lon'}, use_global_device_ids=true, to_apply=%region_7.8 | all-reduce | flops 1625 | bytes 13000 | tf_op jit(solution)/shard_map/psum | solution.py:198
  (305 shorter events, 87.1 us)
Async XLA Ops:
  7.2 29.5 %copy-start = (bf16[16,8,640]{2,1,0:T(8,128)(2,1)S(1)}, bf16[16,8,640]{2,1,0:T(8,128)(2,1)}, u32[]{:S(2)}) copy-start(bf16[16,8,640]{2,1,0:T(8,128)(2,1)} %param.13) | copy-start | bytes 491524
  7.2 29.5 %all-gather.3.cloned.1.call-start = ((), (), s32[]{:S(2)}) async-start(), calls=%async_computation.1 | async-start | bytes 1638400 | tf_op jit(solution)/shard_map/all_gather | solution.py:79
  9.0 230.4 %all-gather.5.cloned.1.call-start = ((), (), s32[]{:S(2)}) async-start(), calls=%async_computation.2 | async-start | bytes 6656000 | tf_op jit(solution)/shard_map/all_gather | solution.py:84
  9.8 917.1 %reduce-scatter.2.cloned.1.call-start = ((), (), s32[]{:S(2)}) async-start(), calls=%async_computation.3 | async-start | bytes 13312000 | tf_op jit(solution)/shard_map/reduce_scatter | solution.py:204
  45.7 4.4 collective-permute-start
  45.8 4.8 collective-permute-start.1
  50.6 5.5 copy-start.1
  51.5 19.0 %collective-permute-start.3 = (bf16[2,28,6,640]{3,0,2,1:T(2,128)(2,1)S(1)}, bf16[2,28,6,640]{3,0,2,1:T(2,128)(2,1)S(1)}, u32[]{:S(2)}, u32[]{:S(2)}) collective-permute-start(bf16[2,28,6,640]{3,0,2,1:T(2,128)(2,1)S(1)} %copy.59), channel_id=1, source_target_pairs={{4,0},{8,4},{12,8},{16,12},{20,16},{24,20},{28,24},{0,28},{5,1},{9... | collective-permute-start | bytes 1290248 | tf_op jit(solution)/shard_map/ppermute | solution.py:18
  56.1 24.7 %collective-permute-start.2 = (bf16[2,28,6,640]{3,0,2,1:T(2,128)(2,1)S(1)}, bf16[2,28,6,640]{3,0,2,1:T(2,128)(2,1)S(1)}, u32[]{:S(2)}, u32[]{:S(2)}) collective-permute-start(bf16[2,28,6,640]{3,0,2,1:T(2,128)(2,1)S(1)} %copy.58), channel_id=1, source_target_pairs={{0,4},{4,8},{8,12},{12,16},{16,20},{20,24},{24,28},{28,0},{1,5},{5... | collective-permute-start | bytes 1290248 | tf_op jit(solution)/shard_map/ppermute | solution.py:17
  80.9 158.5 %copy-start.11 = (bf16[16,8,5120]{2,0,1:T(8,128)(2,1)S(1)}, bf16[16,8,5120]{2,0,1:T(8,128)(2,1)}, u32[]{:S(2)}) copy-start(bf16[16,8,5120]{2,0,1:T(8,128)(2,1)} %all-gather.3.cloned.1.call-done) | copy-start | bytes 3932164
  245.9 13.4 %copy-start.12 = (bf16[16,8,5,128]{3,1,2,0:T(8,128)(2,1)}, bf16[16,8,5,128]{3,1,2,0:T(8,128)(2,1)S(1)}, u32[]{:S(2)}) copy-start(bf16[16,8,5,128]{3,1,2,0:T(8,128)(2,1)S(1)} %get-tuple-element.541) | copy-start | bytes 491524 | tf_op jit(solution)/shard_map/while
  275.2 13.4 %copy-start.12 = (bf16[16,8,5,128]{3,1,2,0:T(8,128)(2,1)}, bf16[16,8,5,128]{3,1,2,0:T(8,128)(2,1)S(1)}, u32[]{:S(2)}) copy-start(bf16[16,8,5,128]{3,1,2,0:T(8,128)(2,1)S(1)} %get-tuple-element.541) | copy-start | bytes 491524 | tf_op jit(solution)/shard_map/while
  304.4 13.4 %copy-start.12 = (bf16[16,8,5,128]{3,1,2,0:T(8,128)(2,1)}, bf16[16,8,5,128]{3,1,2,0:T(8,128)(2,1)S(1)}, u32[]{:S(2)}) copy-start(bf16[16,8,5,128]{3,1,2,0:T(8,128)(2,1)S(1)} %get-tuple-element.541) | copy-start | bytes 491524 | tf_op jit(solution)/shard_map/while
  333.6 13.4 %copy-start.12 = (bf16[16,8,5,128]{3,1,2,0:T(8,128)(2,1)}, bf16[16,8,5,128]{3,1,2,0:T(8,128)(2,1)S(1)}, u32[]{:S(2)}) copy-start(bf16[16,8,5,128]{3,1,2,0:T(8,128)(2,1)S(1)} %get-tuple-element.541) | copy-start | bytes 491524 | tf_op jit(solution)/shard_map/while
  365.3 4.3 copy-start.4
  365.3 4.7 copy-start.14
  367.6 159.4 %collective-permute-start.5 = (bf16[2,28,6,640]{3,0,2,1:T(2,128)(2,1)}, bf16[2,28,6,640]{3,0,2,1:T(2,128)(2,1)}, u32[]{:S(2)}, u32[]{:S(2)}) collective-permute-start(bf16[2,28,6,640]{3,0,2,1:T(2,128)(2,1)} %copy.71), channel_id=1, source_target_pairs={{4,0},{8,4},{12,8},{16,12},{20,16},{24,20},{28,24},{0,28},{5,1},{9... | collective-permute-start | bytes 1290248 | tf_op jit(solution)/shard_map/ppermute | solution.py:18
  367.6 160.5 %collective-permute-start.4 = (bf16[2,28,6,640]{3,0,2,1:T(2,128)(2,1)}, bf16[2,28,6,640]{3,0,2,1:T(2,128)(2,1)}, u32[]{:S(2)}, u32[]{:S(2)}) collective-permute-start(bf16[2,28,6,640]{3,0,2,1:T(2,128)(2,1)} %copy.70), channel_id=1, source_target_pairs={{0,4},{4,8},{8,12},{12,16},{16,20},{20,24},{24,28},{28,0},{1,5},{5... | collective-permute-start | bytes 1290248 | tf_op jit(solution)/shard_map/ppermute | solution.py:17
  529.9 8.9 copy-start.16
  529.9 8.9 copy-start.18
  529.9 8.9 copy-start.20
  532.2 393.8 %copy-start.22 = (pred[16]{0:T(512)(128)(4,1)S(1)}, pred[16]{0:T(512)(128)(4,1)}, u32[]{:S(2)}) copy-start(pred[16]{0:T(512)(128)(4,1)} %constant.227.clone.1) | copy-start | bytes 52
  532.3 393.6 %collective-permute-start.6 = (bf16[2,6,8,640]{3,2,1,0:T(8,128)(2,1)S(1)}, bf16[2,6,8,640]{3,2,1,0:T(8,128)(2,1)S(1)}, u32[]{:S(2)}, u32[]{:S(2)}) collective-permute-start(bf16[2,6,8,640]{3,2,1,0:T(8,128)(2,1)S(1)} %get-tuple-element.361), channel_id=1, source_target_pairs={{0,32},{32,64},{64,96},{96,128},{128,160},{160,192},{192,224},{1,3... | collective-permute-start | bytes 368648 | tf_op jit(solution)/shard_map/ppermute | solution.py:17
  534.3 391.5 %collective-permute-start.7 = (bf16[2,6,8,640]{3,2,1,0:T(8,128)(2,1)S(1)}, bf16[2,6,8,640]{3,2,1,0:T(8,128)(2,1)S(1)}, u32[]{:S(2)}, u32[]{:S(2)}) collective-permute-start(bf16[2,6,8,640]{3,2,1,0:T(8,128)(2,1)S(1)} %get-tuple-element.362), channel_id=1, source_target_pairs={{32,0},{64,32},{96,64},{128,96},{160,128},{192,160},{224,192},{33,... | collective-permute-start | bytes 368648 | tf_op jit(solution)/shard_map/ppermute | solution.py:18
  (22 other events, 43.6 us)
Sparse Core Ops, SparseCore 0:
  9.8 26.8 all-gather.2
  38.5 200.8 all-gather.4
  242.6 461.3 reduce-scatter.1
where the time goes:
time: 935 us; the launch traced here: 933 us
  blocking collectives  386 us (41%)
  local copies, waits for them, and re-layouts  227 us (24%)
  waiting for transfers between devices  207 us (22%)
  loops' own time  33.7 us (4%)
  other arithmetic  28.7 us (3%)
  matrix products  21.7 us (2%)
  starting transfers between devices  15.1 us (2%)
  between operations  14.2 us (2%)
    psum x1, blocking collectives, local(): grad_table = lax.psum(table_local, ('lat', 'lon'))  386 us
    all_gather x1, waiting for transfers between devices, local(): lax.all_gather(w_out, ('lat', 'lon'), axis=0, tiled=True)  156 us
    gather x3, local copies, waits for them, and re-layouts, local(): jnp.take_along_axis(table_core, col_take, axis=3)  156 us
    another operation x1, loops' own time, local(): lax.scan(block_step, (zero_pair, zero_table), jnp.arange(block_count, dty...  33.7 us
    all_gather x1, waiting for transfers between devices, local(): lax.all_gather(grad_out, 'chan', axis=2, tiled=True).reshape(tokens, -1)  26.9 us
  transfers between devices with their start and end apart: 11, of which 6 were waited for; matrix products, arithmetic and copies ran while one was open for 29% of the time, Pallas kernels for 0%

commit v1 on v0

v1 whole, which is shorter than its diff:
```python
import jax
import jax.numpy as jnp
from jax import lax
from jax.experimental import pallas as pl
from jax.experimental.pallas import tpu as pltpu
from jax.sharding import PartitionSpec as P

HEAD_DIM = 128
WIN = 13
REACH = 6
NEG = -1e30
F32 = jnp.float32
BF16 = jnp.bfloat16
SEG_ROWS = 32
ROWS = 16
COLS = 8
EXT_ROWS = ROWS + 2 * REACH
SEG = SEG_ROWS * COLS
USED = EXT_ROWS * COLS
SHIFTED = (SEG_ROWS + ROWS) * COLS


def dot_t0(a, b):
    return lax.dot_general(a, b, (((0,), (0,)), ((), ())), preferred_element_type=F32)


def dot_t1(a, b):
    return lax.dot_general(a, b, (((1,), (1,)), ((), ())), preferred_element_type=F32)


def grad_attn_body(grad_ref, w_ref, out_ref):
    total = dot_t0(grad_ref[0, 0], w_ref[0])
    for c in range(1, grad_ref.shape[0]):
        total = total + dot_t0(grad_ref[c, 0], w_ref[c])
    out_ref[0] = total.astype(BF16)


def grad_attn_parts(grad_feats, w_rows):
    chans, groups, feats, tokens = grad_feats.shape
    width = w_rows.shape[2]
    return pl.pallas_call(
        grad_attn_body,
        grid=(groups,),
        in_specs=[
            pl.BlockSpec((chans, 1, feats, tokens), lambda i: (0, i, 0, 0)),
            pl.BlockSpec((chans, feats, width), lambda i: (0, 0, 0)),
        ],
        out_specs=pl.BlockSpec((1, tokens, width), lambda i: (i, 0, 0)),
        out_shape=jax.ShapeDtypeStruct((groups, tokens, width), BF16),
        name="grad_attn_parts",
    )(grad_feats, w_rows)


def grad_wout_body(grad_ref, attn_ref, out_ref):
    first = pl.program_id(0) == 0
    for c in range(grad_ref.shape[0]):
        part = jnp.dot(grad_ref[c, 0], attn_ref[0], preferred_element_type=F32)

        @pl.when(first)
        def _():
            out_ref[c] = part

        @pl.when(jnp.logical_not(first))
        def _():
            out_ref[c] = out_ref[c] + part


def grad_wout_part(grad_feats, attn_rows):
    chans, groups, feats, tokens = grad_feats.shape
    width = attn_rows.shape[2]
    return pl.pallas_call(
        grad_wout_body,
        grid=(groups,),
        in_specs=[
            pl.BlockSpec((chans, 1, feats, tokens), lambda i: (0, i, 0, 0)),
            pl.BlockSpec((1, tokens, width), lambda i: (i, 0, 0)),
        ],
        out_specs=pl.BlockSpec((chans, feats, width), lambda i: (0, 0, 0)),
        out_shape=jax.ShapeDtypeStruct((chans, feats, width), F32),
        name="grad_wout_part",
    )(grad_feats, attn_rows)


def attn_body(q_ref, part_ref, left_ref, core_ref, right_ref, bias_ref, mask_ref,
              dq_ref, dleft_ref, dcore_ref, dright_ref, table_ref, bias_all):
    scale = HEAD_DIM ** (-0.5)
    tokens = ROWS * COLS
    for i in range(ROWS):
        off = (ROWS - 1 - i) * COLS
        for s in range(3):
            row = bias_ref[0, s]
            if off:
                row = pltpu.roll(row, SHIFTED - off, 1)
            row = row[:, :SEG] + mask_ref[i : i + 1, s * SEG : (s + 1) * SEG]
            bias_all[i * COLS : (i + 1) * COLS, s * SEG : (s + 1) * SEG] = row
    q = q_ref[...]
    do_sum = part_ref[0].astype(F32)
    for g in range(1, part_ref.shape[0]):
        do_sum = do_sum + part_ref[g].astype(F32)
    do = do_sum.astype(BF16)
    fill = jnp.zeros((SEG - USED, HEAD_DIM), BF16)
    k = jnp.concatenate([left_ref[0], fill, core_ref[0], fill, right_ref[0], fill], axis=0)
    v = jnp.concatenate([left_ref[1], fill, core_ref[1], fill, right_ref[1], fill], axis=0)
    scores = dot_t1(q, k) * scale + bias_all[...]
    row_max = jnp.max(scores, axis=1, keepdims=True)
    weights = jnp.exp(scores - row_max)
    probs = weights * (1.0 / jnp.sum(weights, axis=1, keepdims=True))
    grad_probs = dot_t1(do, v)
    delta = jnp.sum(probs * grad_probs, axis=1, keepdims=True)
    dscore = probs * (grad_probs - delta)
    dscore_low = dscore.astype(BF16)
    prob_low = probs.astype(BF16)
    dq_ref[...] = (scale * jnp.dot(dscore_low, k, preferred_element_type=F32)).astype(BF16)
    dk = scale * dot_t0(dscore_low, q)
    dv = dot_t0(prob_low, do)
    for n, part in enumerate((dk, dv)):
        dleft_ref[n] = part[:USED].astype(BF16)
        dcore_ref[n] = part[SEG : SEG + USED]
        dright_ref[n] = part[2 * SEG : 2 * SEG + USED].astype(BF16)
    bias_all[...] = dscore
    tail = jnp.zeros((COLS, SHIFTED - SEG), F32)
    for s in range(3):
        acc = None
        for i in range(ROWS):
            off = (ROWS - 1 - i) * COLS
            piece = bias_all[i * COLS : (i + 1) * COLS, s * SEG : (s + 1) * SEG]
            piece = jnp.concatenate([piece, tail], axis=1)
            if off:
                piece = pltpu.roll(piece, off, 1)
            acc = piece if acc is None else acc + piece
        table_ref[0, s] = acc


def attn_backward(queries, parts, left, core, right, bias_rows, mask):
    tokens, width = queries.shape
    heads = width // HEAD_DIM
    groups = parts.shape[0]
    seg_in = pl.BlockSpec((2, USED, HEAD_DIM), lambda h: (0, 0, h))
    seg_low = jax.ShapeDtypeStruct((2, USED, width), BF16)
    return pl.pallas_call(
        attn_body,
        grid=(heads,),
        in_specs=[
            pl.BlockSpec((tokens, HEAD_DIM), lambda h: (0, h)),
            pl.BlockSpec((groups, tokens, HEAD_DIM), lambda h: (0, 0, h)),
            seg_in,
            seg_in,
            seg_in,
            pl.BlockSpec((1, 3, COLS, SHIFTED), lambda h: (h, 0, 0, 0)),
            pl.BlockSpec((ROWS, 3 * SEG), lambda h: (0, 0)),
        ],
        out_specs=[
            pl.BlockSpec((tokens, HEAD_DIM), lambda h: (0, h)),
            seg_in,
            seg_in,
            seg_in,
            pl.BlockSpec((1, 3, COLS, SHIFTED), lambda h: (h, 0, 0, 0)),
        ],
        out_shape=[
            jax.ShapeDtypeStruct((tokens, width), BF16),
            seg_low,
            jax.ShapeDtypeStruct((2, USED, width), F32),
            seg_low,
            jax.ShapeDtypeStruct((heads, 3, COLS, SHIFTED), F32),
        ],
        scratch_shapes=[pltpu.VMEM((tokens, 3 * SEG), F32)],
        name="attn_backward",
    )(queries, parts, left, core, right, bias_rows, mask)


def shift(value, axis, step, wrap):
    count = lax.axis_size(axis)
    pairs = [
        (i, (i + step) % count) for i in range(count) if wrap or 0 <= i + step < count
    ]
    return lax.ppermute(value, axis, pairs)


def make_mask(key_mask):
    lat_total, lon_total = key_mask.shape
    lat, lon = lax.axis_index("lat"), lax.axis_index("lon")
    rows = lax.broadcasted_iota(jnp.int32, key_mask.shape, 0)
    cols = lax.broadcasted_iota(jnp.int32, key_mask.shape, 1)
    valid = ((key_mask == 1) | ((rows % 4 == 0) & (cols % 4 == 0))).astype(F32)
    valid = jnp.pad(valid, ((REACH, SEG_ROWS - ROWS - REACH), (0, 0)))
    valid = jnp.concatenate([valid[:, -COLS:], valid, valid[:, :COLS]], axis=1)
    valid = lax.dynamic_slice(valid, (lat * ROWS, lon * COLS), (SEG_ROWS, 3 * COLS))
    valid = valid.reshape(SEG_ROWS, 3, COLS).transpose(1, 0, 2).reshape(1, 3 * SEG)
    row_of = (lax.broadcasted_iota(jnp.int32, (ROWS, 3 * SEG), 1) // COLS) % SEG_ROWS
    query = lat * ROWS + lax.broadcasted_iota(jnp.int32, (ROWS, 3 * SEG), 0)
    low = jnp.clip(query - REACH, 0, lat_total - WIN) - lat * ROWS + REACH
    allowed = (row_of >= low) & (row_of < low + WIN) & (valid > 0)
    return jnp.where(allowed, 0.0, NEG).astype(F32)


def spread_bias(table):
    heads, offsets, _ = table.shape
    pad_y = COLS + 1
    padded = jnp.pad(
        table,
        ((0, 0), (ROWS - 1 - REACH, SEG_ROWS + ROWS - offsets - (ROWS - 1 - REACH)), (pad_y, pad_y)),
        constant_values=NEG,
    )
    pieces = []
    for s in range(3):
        for j in range(COLS):
            first = COLS * (s - 1) - j + REACH + pad_y
            pieces.append(padded[:, :, first : first + COLS])
    return jnp.stack(pieces, axis=1).reshape(heads, 3, COLS, SHIFTED)


def gather_table(spread):
    heads = spread.shape[0]
    offsets = 2 * WIN - 1
    first_row = ROWS - 1 - REACH
    grid = spread.reshape(heads, 3, COLS, SEG_ROWS + ROWS, COLS)[:, :, :, first_row : first_row + offsets]
    pad_y = COLS + 1
    total = jnp.zeros((heads, offsets, WIN + 2 * pad_y), F32)
    for s in range(3):
        for j in range(COLS):
            first = COLS * (s - 1) - j + REACH + pad_y
            total = total + jnp.pad(
                grid[:, s, j], ((0, 0), (0, 0), (first, WIN + 2 * pad_y - COLS - first))
            )
    return total[:, :, pad_y : pad_y + WIN]


def local(queries, keys, values, attn_out, grad_out, w_out, bias_table, key_mask):
    lat_rows, lon_cols, width = queries.shape
    tokens = lat_rows * lon_cols
    feats_local = grad_out.shape[2]
    lon_n = lax.axis_size("lon")
    lat_n = lax.axis_size("lat")
    chan_n = lax.axis_size("chan")
    w_rows_local = w_out.shape[0]
    per_chan = feats_local // (lon_n * w_rows_local)

    kv = jnp.stack([keys, values])
    above = shift(kv[:, lat_rows - REACH :], "lat", 1, False)
    below = shift(kv[:, :REACH], "lat", -1, False)

    grad_t = grad_out.reshape(tokens, feats_local).T
    grad_t = grad_t.reshape(per_chan, lon_n, w_rows_local, tokens).transpose(1, 0, 2, 3)
    grad_t = grad_t.reshape(lon_n, per_chan * w_rows_local, tokens)
    grad_x = lax.all_to_all(grad_t, "lon", 0, 0)
    grad_feats = lax.all_to_all(
        jnp.broadcast_to(grad_x[None], (chan_n, *grad_x.shape)), "chan", 0, 0
    )
    w_rows = lax.all_gather(w_out, "lat", axis=0).reshape(
        chan_n, per_chan * w_rows_local, width
    )
    attn_rows = lax.all_gather(attn_out.reshape(tokens, width), "lon", axis=0)

    core = jnp.concatenate([above, kv, below], axis=1).reshape(2, USED, width)
    left = shift(core, "lon", 1, True)
    right = shift(core, "lon", -1, True)

    parts = lax.all_to_all(grad_attn_parts(grad_feats, w_rows), "lon", 0, 0)

    wout_part = grad_wout_part(grad_feats, attn_rows).reshape(lat_n * w_rows_local, width)
    grad_wout = lax.psum_scatter(wout_part, "lat", scatter_dimension=0, tiled=True)

    dq, dleft, dcore, dright, spread = attn_backward(
        queries.reshape(tokens, width),
        parts,
        left,
        core,
        right,
        spread_bias(bias_table),
        make_mask(key_mask),
    )
    from_right = shift(dleft, "lon", -1, True)
    from_left = shift(dright, "lon", 1, True)
    table = gather_table(spread)
    table = jnp.pad(table.reshape(-1), (0, -table.size % 1024)).reshape(-1, 128)
    table = jnp.sum(lax.all_to_all(jnp.broadcast_to(table[None], (lat_n, *table.shape)), "lat", 0, 0), axis=0)
    folded = dcore + from_right.astype(F32) + from_left.astype(F32)
    edge = REACH * COLS
    from_below = shift(folded[:, :edge].astype(BF16), "lat", -1, False)
    from_above = shift(folded[:, USED - edge :].astype(BF16), "lat", 1, False)
    table = jnp.sum(lax.all_to_all(jnp.broadcast_to(table[None], (lon_n, *table.shape)), "lon", 0, 0), axis=0)
    grad_table = table.reshape(-1)[: bias_table.size].reshape(bias_table.shape)
    folded = folded[:, edge : USED - edge]
    folded = folded + jnp.pad(from_above.astype(F32), ((0, 0), (0, tokens - edge), (0, 0)))
    folded = folded + jnp.pad(from_below.astype(F32), ((0, 0), (tokens - edge, 0), (0, 0)))
    folded = folded.astype(BF16).reshape(2, lat_rows, lon_cols, width)
    return (
        dq.reshape(lat_rows, lon_cols, width),
        folded[0],
        folded[1],
        grad_wout,
        grad_table,
    )


def solution(mesh):
    return jax.shard_map(
        local,
        mesh=mesh,
        in_specs=(
            P("lat", "lon", "chan"),
            P("lat", "lon", "chan"),
            P("lat", "lon", "chan"),
            P("lat", "lon", "chan"),
            P("lat", "lon", "chan"),
            P(("lat", "lon"), "chan"),
            P("chan", None, None),
            P(),
        ),
        out_specs=(
            P("lat", "lon", "chan"),
            P("lat", "lon", "chan"),
            P("lat", "lon", "chan"),
            P(("lat", "lon"), "chan"),
            P("chan", None, None),
        ),
        check_vma=False,
    )
```

time: 935 us -> 230 us (0.25)
  the two profiles are of different devices: /device:TPU:240 before, /device:TPU:32 now
where the time goes in v1:
time: 230 us; the launch traced here: 228 us
  waiting for transfers between devices  81.5 us (35%)
  starting transfers between devices  46 us (20%)
  blocking collectives  42.3 us (18%)
  Pallas kernels  24.3 us (11%)
  local copies, waits for them, and re-layouts  16.1 us (7%)
  between operations  14.3 us (6%)
  other arithmetic  4.02 us (2%)
    ppermute x8, waiting for transfers between devices, shift(): return lax.ppermute(value, axis, pairs)  63 us
    all_to_all x1, blocking collectives, local(): lax.all_to_all(jnp.broadcast_to(table[None], (lon_n, *table.shape)), 'lon...  23.1 us
    ppermute x8, starting transfers between devices, shift(): return lax.ppermute(value, axis, pairs)  20.2 us
    all_gather x1, blocking collectives, local(): lax.all_gather(w_out, 'lat', axis=0)  19.2 us
    all_to_all x1, waiting for transfers between devices, local(): grad_x = lax.all_to_all(grad_t, 'lon', 0, 0)  16.7 us
    all_to_all x1, starting transfers between devices, local(): grad_x = lax.all_to_all(grad_t, 'lon', 0, 0)  10 us
    pallas_call x1, Pallas kernels, grad_wout_part(): pl.pallas_call(grad_wout_body, grid=(groups,), in_specs=[pl.BlockSpec((ch...  10 us
    pallas_call x1, Pallas kernels, grad_attn_parts(): pl.pallas_call(grad_attn_body, grid=(groups,), in_specs=[pl.BlockSpec((ch...  7.2 us
  transfers between devices with their start and end apart: 14, of which 6 were waited for; matrix products, arithmetic and copies ran while one was open for 8% of the time, Pallas kernels for 11%

profile of v1, /device:TPU:32, one launch (start us, length us, event | category | flops | bytes accessed | tf_op | source)
XLA Modules:
  0.0 228.5 jit_solution(10012033728252075339)
XLA Ops:
  8.9 1.9 collective-permute-start
  10.8 3.6 %collective-permute-start.1 = (bf16[2,6,8,640]{3,2,1,0:T(8,128)(2,1)S(1)}, bf16[2,6,8,640]{3,2,1,0:T(8,128)(2,1)S(1)}, u32[]{:S(2)}, u32[]{:S(2)}) collective-permute-start(bf16[2,6,8,640]{3,2,1,0:T(8,128)(2,1)S(1)} %get-tuple-element.66), channel_id=1, source_target_pairs={{32,0},{64,32},{96,64},{128,96},{160,128},{192,160},{224,192},{33,... | collective-permute-start | bytes 368648 | tf_op jit(solution)/shard_map/ppermute | solution.py:176
  16.4 10.0 %all-to-all-start = ((bf16[8,160,128]{2,1,0:T(8,128)(2,1)}), bf16[8,160,128]{2,1,0:T(8,128)(2,1)S(1)}, u32[]{:S(2)}, u32[]{:S(2)}) async-start(bf16[8,160,128]{2,1,0:T(8,128)(2,1)} %bitcast.5), calls=%async_computation | async-start | bytes 655360 | tf_op jit(solution)/shard_map/all_to_all | solution.py:245
  27.2 16.7 %all-to-all-done = bf16[8,160,128]{2,1,0:T(8,128)(2,1)S(1)} async-done(((bf16[8,160,128]{2,1,0:T(8,128)(2,1)}), bf16[8,160,128]{2,1,0:T(8,128)(2,1)S(1)}, u32[]{:S(2)}, u32[]{:S(2)}) %all-to-all-start) | async-done | bytes 327712 | tf_op jit(solution)/shard_map/all_to_all | solution.py:245
  43.8 1.3 broadcast_in_dim.27
  45.1 4.3 %all-to-all-start.1 = ((bf16[4,8,160,128]{3,2,1,0:T(8,128)(2,1)}), bf16[4,8,160,128]{3,2,1,0:T(8,128)(2,1)S(1)}, u32[]{:S(2)}, u32[]{:S(2)}) async-start(bf16[4,8,160,128]{3,2,1,0:T(8,128)(2,1)} %broadcast_in_dim.27), calls=%async_computation.1 | async-start | bytes 2621440 | tf_op jit(solution)/shard_map/all_to_all | solution.py:246
  49.8 19.2 %all-gather = bf16[640,640]{1,0:T(8,128)(2,1)} all-gather(bf16[80,640]{1,0:T(8,128)(2,1)S(1)} %copy-done.7), channel_id=2, replica_groups=mesh['lat'=8,'lon'=8,'chan'=4] {'lat'}, dimensions={0}, use_global_device_ids=true | all-gather | bytes 921600 | tf_op jit(solution)/shard_map/all_gather | solution.py:249
  70.1 7.2 %grad_attn_parts.1 = bf16[8,128,640]{2,1,0:T(8,128)(2,1)} custom-call(bf16[4,8,160,128]{3,2,1,0:T(8,128)(2,1)} %copy-done.1, bf16[4,160,640]{2,1,0:T(8,128)(2,1)} %bitcast.206), custom_call_target="tpu_custom_call" | custom-call | tf_op jit(solution)/shard_map/grad_attn_parts/pallas_call | solution.py:41
  77.3 4.4 %all-to-all-start.2 = ((bf16[8,128,640]{2,1,0:T(8,128)(2,1)}), bf16[8,128,640]{2,1,0:T(8,128)(2,1)}, u32[]{:S(2)}, u32[]{:S(2)}) async-start(bf16[8,128,640]{2,1,0:T(8,128)(2,1)} %grad_attn_parts.1), calls=%async_computation.2 | async-start | bytes 2621440 | tf_op jit(solution)/shard_map/all_to_all | solution.py:258
  83.2 10.0 %grad_wout_part.1 = f32[4,160,640]{2,1,0:T(8,128)} custom-call(bf16[4,8,160,128]{3,2,1,0:T(8,128)(2,1)} %copy-done.1, bf16[8,128,640]{2,1,0:T(8,128)(2,1)} %all-gather.3.cloned.1.call-done.attn_ref), custom_call_target="tpu_custom_call" | custom-call | tf_op jit(solution)/shard_map/grad_wout_part/pallas_call | solution.py:71
  94.4 6.9 %collective-permute-start.3 = (bf16[2,224,640]{2,1,0:T(8,128)(2,1)S(1)}, bf16[2,224,640]{2,1,0:T(8,128)(2,1)}, u32[]{:S(2)}, u32[]{:S(2)}) collective-permute-start(bf16[2,224,640]{2,1,0:T(8,128)(2,1)S(1)} %maximum_bitcast_fusion.core_ref), channel_id=1, source_target_pairs={{0,28},{4,0},{8,4},{12,8},{16,12},{20,16},{24,20},{28,24},{1,29},{... | collective-permute-start | bytes 1720328 | tf_op jit(solution)/shard_map/ppermute | solution.py:176
  101.6 1.9 copy.123
  103.5 2.1 reshape.76.bias_ref
  106.4 40.3 %collective-permute-done.3.right_ref = bf16[2,224,640]{2,1,0:T(8,128)(2,1)} collective-permute-done((bf16[2,224,640]{2,1,0:T(8,128)(2,1)S(1)}, bf16[2,224,640]{2,1,0:T(8,128)(2,1)}, u32[]{:S(2)}, u32[]{:S(2)}) %collective-permute-start.3) | collective-permute-done | bytes 573472 | tf_op jit(solution)/shard_map/ppermute | solution.py:176
  146.7 10.3 %collective-permute-done.2.left_ref = bf16[2,224,640]{2,1,0:T(8,128)(2,1)} collective-permute-done((bf16[2,224,640]{2,1,0:T(8,128)(2,1)S(1)}, bf16[2,224,640]{2,1,0:T(8,128)(2,1)}, u32[]{:S(2)}, u32[]{:S(2)}) %collective-permute-start.2) | collective-permute-done | bytes 573472 | tf_op jit(solution)/shard_map/ppermute | solution.py:176
  156.9 7.1 %attn_backward.1 = (bf16[128,640]{1,0:T(8,128)(2,1)}, bf16[2,224,640]{2,1,0:T(8,128)(2,1)}, f32[2,224,640]{2,1,0:T(8,128)}, bf16[2,224,640]{2,1,0:T(8,128)(2,1)}, f32[5,3,8,384]{3,2,1,0:T(8,128)}) custom-call(bf16[128,640]{1,0:T(8,128)(2,1)} %bitcast.214, bf16[8,128,640]{2,1,0:T(8,128)(2,1)} %all-to-all-done.2.part_ref, ...), custom_call_target="tpu_custom_call" | custom-call | tf_op jit(solution)/shard_map/attn_backward/pallas_call | solution.py:140
  164.1 2.0 collective-permute-start.5
  166.1 2.5 %reshape.79 = f32[5,3,8,48,8]{4,3,2,1,0:T(8,128)S(1)} reshape(f32[5,3,8,384]{3,2,1,0:T(8,128)} %get-tuple-element.14) | data formatting | bytes 368640 | tf_op jit(solution)/shard_map/reshape | solution.py:216
  170.5 7.0 %all-to-all-start.3 = ((f32[8,16,128]{2,1,0:T(8,128)}), f32[8,16,128]{2,1,0:T(8,128)S(1)}, u32[]{:S(2)}, u32[]{:S(2)}) async-start(f32[8,16,128]{2,1,0:T(8,128)} %broadcast_in_dim.31), calls=%async_computation.4 | async-start | bytes 131072 | tf_op jit(solution)/shard_map/all_to_all | solution.py:276
  177.5 3.9 %collective-permute-done.4 = bf16[2,224,640]{2,1,0:T(8,128)(2,1)S(1)} collective-permute-done((bf16[2,224,640]{2,1,0:T(8,128)(2,1)}, bf16[2,224,640]{2,1,0:T(8,128)(2,1)S(1)}, u32[]{:S(2)}, u32[]{:S(2)}) %collective-permute-start.4) | collective-permute-done | bytes 573472 | tf_op jit(solution)/shard_map/ppermute | solution.py:176
  181.4 8.5 %collective-permute-done.5 = bf16[2,224,640]{2,1,0:T(8,128)(2,1)} collective-permute-done((bf16[2,224,640]{2,1,0:T(8,128)(2,1)}, bf16[2,224,640]{2,1,0:T(8,128)(2,1)}, u32[]{:S(2)}, u32[]{:S(2)}) %collective-permute-start.5) | collective-permute-done | bytes 573472 | tf_op jit(solution)/shard_map/ppermute | solution.py:176
  191.2 1.9 collective-permute-start.6
  193.1 3.6 %collective-permute-start.7 = (bf16[2,48,640]{2,1,0:T(8,128)(2,1)S(1)}, bf16[2,48,640]{2,1,0:T(8,128)(2,1)S(1)}, u32[]{:S(2)}, u32[]{:S(2)}) collective-permute-start(bf16[2,48,640]{2,1,0:T(8,128)(2,1)S(1)} %get-tuple-element.62), channel_id=1, source_target_pairs={{32,0},{64,32},{96,64},{128,96},{160,128},{192,160},{224,192},{33,... | collective-permute-start | bytes 368648 | tf_op jit(solution)/shard_map/ppermute | solution.py:176
  196.8 23.1 %all_to_all.25 = f32[8,16,128]{2,1,0:T(8,128)S(1)} all-to-all(f32[8,16,128]{2,1,0:T(8,128)S(1)} %broadcast_in_dim.32), channel_id=1, replica_groups=mesh['lat'=8,'lon'=8,'chan'=4] {'lon'}, dimensions={0} | all-to-all | bytes 131072 | tf_op jit(solution)/shard_map/all_to_all | solution.py:281
  (91 shorter events, 14.3 us)
Async XLA Ops:
  7.2 76.1 %all-gather.3.cloned.1.call-start = ((), (), s32[]{:S(2)}) async-start(), calls=%async_computation.6 | async-start | bytes 1474560 | tf_op jit(solution)/shard_map/all_gather | solution.py:252
  7.9 18.5 %copy-start = (f32[5,25,13]{1,2,0:T(8,128)S(1)}, f32[5,25,13]{1,2,0:T(8,128)}, u32[]{:S(2)}) copy-start(f32[5,25,13]{1,2,0:T(8,128)} %param.14) | copy-start | bytes 19504
  8.9 84.7 %collective-permute-start = (bf16[2,6,8,640]{3,2,1,0:T(8,128)(2,1)S(1)}, bf16[2,6,8,640]{3,2,1,0:T(8,128)(2,1)S(1)}, u32[]{:S(2)}, u32[]{:S(2)}) collective-permute-start(bf16[2,6,8,640]{3,2,1,0:T(8,128)(2,1)S(1)} %get-tuple-element.65), channel_id=1, source_target_pairs={{0,32},{32,64},{64,96},{96,128},{128,160},{160,192},{192,224},{1,3... | collective-permute-start | bytes 368648 | tf_op jit(solution)/shard_map/ppermute | solution.py:176
  10.8 82.8 %collective-permute-start.1 = (bf16[2,6,8,640]{3,2,1,0:T(8,128)(2,1)S(1)}, bf16[2,6,8,640]{3,2,1,0:T(8,128)(2,1)S(1)}, u32[]{:S(2)}, u32[]{:S(2)}) collective-permute-start(bf16[2,6,8,640]{3,2,1,0:T(8,128)(2,1)S(1)} %get-tuple-element.66), channel_id=1, source_target_pairs={{32,0},{64,32},{96,64},{128,96},{160,128},{192,160},{224,192},{33,... | collective-permute-start | bytes 368648 | tf_op jit(solution)/shard_map/ppermute | solution.py:176
  16.4 27.4 %all-to-all-start = ((bf16[8,160,128]{2,1,0:T(8,128)(2,1)}), bf16[8,160,128]{2,1,0:T(8,128)(2,1)S(1)}, u32[]{:S(2)}, u32[]{:S(2)}) async-start(bf16[8,160,128]{2,1,0:T(8,128)(2,1)} %bitcast.5), calls=%async_computation | async-start | bytes 655360 | tf_op jit(solution)/shard_map/all_to_all | solution.py:245
  45.1 4.7 %copy-start.7 = (bf16[80,640]{1,0:T(8,128)(2,1)S(1)}, bf16[80,640]{1,0:T(8,128)(2,1)}, u32[]{:S(2)}) copy-start(bf16[80,640]{1,0:T(8,128)(2,1)} %param.13) | copy-start | bytes 307204
  45.1 23.9 %all-to-all-start.1 = ((bf16[4,8,160,128]{3,2,1,0:T(8,128)(2,1)}), bf16[4,8,160,128]{3,2,1,0:T(8,128)(2,1)S(1)}, u32[]{:S(2)}, u32[]{:S(2)}) async-start(bf16[4,8,160,128]{3,2,1,0:T(8,128)(2,1)} %broadcast_in_dim.27), calls=%async_computation.1 | async-start | bytes 2621440 | tf_op jit(solution)/shard_map/all_to_all | solution.py:246
  69.0 1.1 copy-start.1
  77.3 4.7 %copy-start.8 = (s32[128,64]{0,1:T(8,128)S(1)}, s32[128,64]{0,1:T(8,128)}, u32[]{:S(2)}) copy-start(s32[128,64]{0,1:T(8,128)} %param.15) | copy-start | bytes 98308
  77.3 79.6 %all-to-all-start.2 = ((bf16[8,128,640]{2,1,0:T(8,128)(2,1)}), bf16[8,128,640]{2,1,0:T(8,128)(2,1)}, u32[]{:S(2)}, u32[]{:S(2)}) async-start(bf16[8,128,640]{2,1,0:T(8,128)(2,1)} %grad_attn_parts.1), calls=%async_computation.2 | async-start | bytes 2621440 | tf_op jit(solution)/shard_map/all_to_all | solution.py:258
  81.7 139.9 %reduce-scatter.2.cloned.1.call-start = ((), (), s32[]{:S(2)}) async-start(), calls=%async_computation.7 | async-start | bytes 1843200 | tf_op jit(solution)/shard_map/reduce_scatter | solution.py:261
  93.3 0.9 copy-start.4
  93.3 1.0 copy-start.5
  93.6 7.9 %copy-start.6 = (f32[5,24,48,8]{2,3,0,1:T(8,128)}, f32[5,24,48,8]{2,3,0,1:T(8,128)S(1)}, u32[]{:S(2)}) copy-start(f32[5,24,48,8]{2,3,0,1:T(8,128)S(1)} %constant_dynamic-update-slice_fusion) | copy-start | bytes 552964
  94.3 9.2 %copy-start.2 = (bf16[2,224,640]{2,1,0:T(8,128)(2,1)}, bf16[2,224,640]{2,1,0:T(8,128)(2,1)S(1)}, u32[]{:S(2)}) copy-start(bf16[2,224,640]{2,1,0:T(8,128)(2,1)S(1)} %maximum_bitcast_fusion.core_ref) | copy-start | bytes 1720324
  94.4 52.3 %collective-permute-start.3 = (bf16[2,224,640]{2,1,0:T(8,128)(2,1)S(1)}, bf16[2,224,640]{2,1,0:T(8,128)(2,1)}, u32[]{:S(2)}, u32[]{:S(2)}) collective-permute-start(bf16[2,224,640]{2,1,0:T(8,128)(2,1)S(1)} %maximum_bitcast_fusion.core_ref), channel_id=1, source_target_pairs={{0,28},{4,0},{8,4},{12,8},{16,12},{20,16},{24,20},{28,24},{1,29},{... | collective-permute-start | bytes 1720328 | tf_op jit(solution)/shard_map/ppermute | solution.py:176
  101.3 55.6 %collective-permute-start.2 = (bf16[2,224,640]{2,1,0:T(8,128)(2,1)S(1)}, bf16[2,224,640]{2,1,0:T(8,128)(2,1)}, u32[]{:S(2)}, u32[]{:S(2)}) collective-permute-start(bf16[2,224,640]{2,1,0:T(8,128)(2,1)S(1)} %maximum_bitcast_fusion.core_ref), channel_id=1, source_target_pairs={{0,4},{4,8},{8,12},{12,16},{16,20},{20,24},{24,28},{28,0},{1,5},{5... | collective-permute-start | bytes 1720328 | tf_op jit(solution)/shard_map/ppermute | solution.py:176
  164.0 17.3 %collective-permute-start.4 = (bf16[2,224,640]{2,1,0:T(8,128)(2,1)}, bf16[2,224,640]{2,1,0:T(8,128)(2,1)S(1)}, u32[]{:S(2)}, u32[]{:S(2)}) collective-permute-start(bf16[2,224,640]{2,1,0:T(8,128)(2,1)} %get-tuple-element.12), channel_id=1, source_target_pairs={{0,28},{4,0},{8,4},{12,8},{16,12},{20,16},{24,20},{28,24},{1,29},{... | collective-permute-start | bytes 1720328 | tf_op jit(solution)/shard_map/ppermute | solution.py:176
  164.1 25.8 %collective-permute-start.5 = (bf16[2,224,640]{2,1,0:T(8,128)(2,1)}, bf16[2,224,640]{2,1,0:T(8,128)(2,1)}, u32[]{:S(2)}, u32[]{:S(2)}) collective-permute-start(bf16[2,224,640]{2,1,0:T(8,128)(2,1)} %get-tuple-element.13), channel_id=1, source_target_pairs={{0,4},{4,8},{8,12},{12,16},{16,20},{20,24},{24,28},{28,0},{1,5},{5... | collective-permute-start | bytes 1720328 | tf_op jit(solution)/shard_map/ppermute | solution.py:176
  169.0 20.9 %copy-start.3 = (f32[2,224,640]{2,1,0:T(8,128)S(1)}, f32[2,224,640]{2,1,0:T(8,128)}, u32[]{:S(2)}) copy-start(f32[2,224,640]{2,1,0:T(8,128)} %get-tuple-element.11) | copy-start | bytes 3440644
  170.5 26.3 %all-to-all-start.3 = ((f32[8,16,128]{2,1,0:T(8,128)}), f32[8,16,128]{2,1,0:T(8,128)S(1)}, u32[]{:S(2)}, u32[]{:S(2)}) async-start(f32[8,16,128]{2,1,0:T(8,128)} %broadcast_in_dim.31), calls=%async_computation.4 | async-start | bytes 131072 | tf_op jit(solution)/shard_map/all_to_all | solution.py:276
  191.2 29.7 %collective-permute-start.6 = (bf16[2,48,640]{2,1,0:T(8,128)(2,1)S(1)}, bf16[2,48,640]{2,1,0:T(8,128)(2,1)S(1)}, u32[]{:S(2)}, u32[]{:S(2)}) collective-permute-start(bf16[2,48,640]{2,1,0:T(8,128)(2,1)S(1)} %get-tuple-element.61), channel_id=1, source_target_pairs={{0,32},{32,64},{64,96},{96,128},{128,160},{160,192},{192,224},{1,3... | collective-permute-start | bytes 368648 | tf_op jit(solution)/shard_map/ppermute | solution.py:176
  193.1 27.7 %collective-permute-start.7 = (bf16[2,48,640]{2,1,0:T(8,128)(2,1)S(1)}, bf16[2,48,640]{2,1,0:T(8,128)(2,1)S(1)}, u32[]{:S(2)}, u32[]{:S(2)}) collective-permute-start(bf16[2,48,640]{2,1,0:T(8,128)(2,1)S(1)} %get-tuple-element.62), channel_id=1, source_target_pairs={{32,0},{64,32},{96,64},{128,96},{160,128},{192,160},{224,192},{33,... | collective-permute-start | bytes 368648 | tf_op jit(solution)/shard_map/ppermute | solution.py:176
Sparse Core Ops, SparseCore 0:
  10.6 72.6 all-gather.2
  93.4 59.8 reduce-scatter.1

commit v2 on v1

v2 whole, which is shorter than its diff:
```python
import jax
import jax.numpy as jnp
from jax import lax
from jax.experimental import pallas as pl
from jax.experimental.pallas import tpu as pltpu
from jax.sharding import PartitionSpec as P

HEAD_DIM = 128
WIN = 13
LON = ("zh", "x")
LAT = ("zl", "core")
RING = ("zh", "zl")
REACH = 6
NEG = -1e30
F32 = jnp.float32
BF16 = jnp.bfloat16
SEG_ROWS = 32
ROWS = 16
COLS = 8
EXT_ROWS = ROWS + 2 * REACH
SEG = SEG_ROWS * COLS
USED = EXT_ROWS * COLS
EDGE = REACH * COLS
SHIFTED = (SEG_ROWS + ROWS) * COLS


def dot_t0(a, b):
    return lax.dot_general(a, b, (((0,), (0,)), ((), ())), preferred_element_type=F32)


def dot_t1(a, b):
    return lax.dot_general(a, b, (((1,), (1,)), ((), ())), preferred_element_type=F32)


def grad_attn_body(core_ref, grad_ref, own_ref, other_ref, out_ref):
    core = core_ref[0]
    chans, rows = grad_ref.shape[1], grad_ref.shape[3] // 2
    total = None
    for w_ref, pick in ((own_ref, core), (other_ref, 1 - core)):
        grads = [grad_ref[0, c, pick] for c in range(chans)]
        grads = jnp.concatenate(
            [g[z * rows : (z + 1) * rows] for z in range(2) for g in grads], axis=0
        )
        part = dot_t0(grads, w_ref[...])
        total = part if total is None else total + part
    out_ref[0] = total.astype(BF16)


def grad_attn_parts(grad_feats, w_own, w_other, core):
    groups, chans, cores, feats, tokens = grad_feats.shape
    width = w_own.shape[1]
    w_spec = pl.BlockSpec(w_own.shape, lambda i, _: (0, 0))
    return pl.pallas_call(
        grad_attn_body,
        grid_spec=pltpu.PrefetchScalarGridSpec(
            num_scalar_prefetch=1,
            grid=(groups,),
            in_specs=[
                pl.BlockSpec((1, chans, cores, feats, tokens), lambda i, _: (i, 0, 0, 0, 0)),
                w_spec,
                w_spec,
            ],
            out_specs=pl.BlockSpec((1, tokens, width), lambda i, _: (i, 0, 0)),
        ),
        out_shape=jax.ShapeDtypeStruct((groups, tokens, width), BF16),
        name="grad_attn_parts",
    )(core, grad_feats, w_own, w_other)


def grad_wout_body(place_ref, grad_ref, *refs):
    attn_refs, (mine_ref, other_ref) = refs[:-2], refs[-2:]
    groups = grad_ref.shape[0]
    core, x = place_ref[0], place_ref[1]
    attn = jnp.concatenate([ref[...] for ref in attn_refs], axis=0)
    for out_ref, pick in ((mine_ref, core), (other_ref, 1 - core)):
        grads = jnp.concatenate(
            [grad_ref[(x + groups - r) % groups, 0, pick] for r in range(groups)], axis=1
        )
        part = jnp.dot(grads, attn, preferred_element_type=F32)
        rows = out_ref.shape[2]
        for z in range(2):
            out_ref[z, 0] = part[z * rows : (z + 1) * rows].astype(out_ref.dtype)


def grad_wout_parts(grad_feats, attn_rows, place):
    groups, chans, cores, feats, tokens = grad_feats.shape
    width = attn_rows[0].shape[1]
    out_spec = pl.BlockSpec((2, 1, feats // 2, width), lambda c, _: (0, c, 0, 0))
    attn_spec = pl.BlockSpec((tokens, width), lambda c, _: (0, 0))
    return pl.pallas_call(
        grad_wout_body,
        grid_spec=pltpu.PrefetchScalarGridSpec(
            num_scalar_prefetch=1,
            grid=(chans,),
            in_specs=[
                pl.BlockSpec((groups, 1, cores, feats, tokens), lambda c, _: (0, c, 0, 0, 0)),
            ]
            + [attn_spec] * groups,
            out_specs=[out_spec, out_spec],
        ),
        out_shape=[
            jax.ShapeDtypeStruct((2, chans, feats // 2, width), F32),
            jax.ShapeDtypeStruct((2, chans, feats // 2, width), BF16),
        ],
        name="grad_wout_parts",
    )(place, grad_feats, *attn_rows)


def spread_rows(halves):
    shape = (COLS, SHIFTED)
    low = jnp.broadcast_to(halves[0:1], shape)
    high = jnp.broadcast_to(halves[1:2], shape)
    lane = lax.broadcasted_iota(jnp.int32, shape, 1) % COLS
    rel = lane - lax.broadcasted_iota(jnp.int32, shape, 0) - (COLS - REACH)

    def turn(value, first):
        if first < 0:
            value = pltpu.roll(value, first % SHIFTED, 1)
        return pltpu.roll(value, max(first, 0), 1, stride=1, stride_axis=0)

    skip = COLS - REACH
    none = jnp.full(shape, NEG, F32)
    return (
        jnp.where(rel >= 0, turn(low, skip), none),
        jnp.where(rel >= 0, turn(high, skip), jnp.where(rel >= -COLS, turn(low, skip - COLS), none)),
        jnp.where(
            rel >= 0,
            none,
            jnp.where(rel >= -COLS, turn(high, skip - COLS), turn(low, skip - 2 * COLS)),
        ),
    )


def attn_body(q_ref, part_ref, above_ref, mid_ref, below_ref, bias_ref, mask_ref,
              dq_ref, dabove_ref, dmid_ref, dbelow_ref, table_ref, bias_all):
    scale = HEAD_DIM ** (-0.5)
    tokens = ROWS * COLS
    spread = spread_rows(bias_ref[0])
    for i in range(ROWS):
        off = (ROWS - 1 - i) * COLS
        for s in range(3):
            row = spread[s]
            if off:
                row = pltpu.roll(row, SHIFTED - off, 1)
            row = row[:, :SEG] + mask_ref[i : i + 1, s * SEG : (s + 1) * SEG]
            bias_all[i * COLS : (i + 1) * COLS, s * SEG : (s + 1) * SEG] = row
    q = q_ref[...]
    do_sum = part_ref[0].astype(F32)
    for g in range(1, part_ref.shape[0]):
        do_sum = do_sum + part_ref[g].astype(F32)
    do = do_sum.astype(BF16)
    fill = jnp.zeros((SEG - USED, HEAD_DIM), BF16)
    k, v = (
        jnp.concatenate(
            [
                piece
                for s in range(3)
                for piece in (above_ref[n, s], mid_ref[n, s], below_ref[n, s], fill)
            ],
            axis=0,
        )
        for n in range(2)
    )
    scores = dot_t1(q, k) * scale + bias_all[...]
    row_max = jnp.max(scores, axis=1, keepdims=True)
    weights = jnp.exp(scores - row_max)
    probs = weights * (1.0 / jnp.sum(weights, axis=1, keepdims=True))
    grad_probs = dot_t1(do, v)
    delta = jnp.sum(probs * grad_probs, axis=1, keepdims=True)
    dscore = probs * (grad_probs - delta)
    dscore_low = dscore.astype(BF16)
    prob_low = probs.astype(BF16)
    dq_ref[...] = (scale * jnp.dot(dscore_low, k, preferred_element_type=F32)).astype(BF16)
    dk = scale * dot_t0(dscore_low, q)
    dv = dot_t0(prob_low, do)
    for n, part in enumerate((dk, dv)):
        for s in range(3):
            first = s * SEG
            dabove_ref[n, s] = part[first : first + EDGE].astype(BF16)
            dmid_ref[n, s] = part[first + EDGE : first + EDGE + tokens]
            dbelow_ref[n, s] = part[first + EDGE + tokens : first + USED].astype(BF16)
    bias_all[...] = dscore
    tail = jnp.zeros((COLS, SHIFTED - SEG), F32)
    for s in range(3):
        acc = None
        for i in range(ROWS):
            off = (ROWS - 1 - i) * COLS
            piece = bias_all[i * COLS : (i + 1) * COLS, s * SEG : (s + 1) * SEG]
            piece = jnp.concatenate([piece, tail], axis=1)
            if off:
                piece = pltpu.roll(piece, off, 1)
            acc = piece if acc is None else acc + piece
        table_ref[0, s] = acc


def attn_backward(queries, parts, above, mid, below, bias_rows, mask):
    tokens, width = queries.shape
    heads = width // HEAD_DIM
    groups = parts.shape[0]
    edge_spec = pl.BlockSpec((2, 3, EDGE, HEAD_DIM), lambda h: (0, 0, 0, h))
    mid_spec = pl.BlockSpec((2, 3, tokens, HEAD_DIM), lambda h: (0, 0, 0, h))
    edge_low = jax.ShapeDtypeStruct((2, 3, EDGE, width), BF16)
    return pl.pallas_call(
        attn_body,
        grid=(heads,),
        in_specs=[
            pl.BlockSpec((tokens, HEAD_DIM), lambda h: (0, h)),
            pl.BlockSpec((groups, tokens, HEAD_DIM), lambda h: (0, 0, h)),
            edge_spec,
            mid_spec,
            edge_spec,
            pl.BlockSpec((1, 2, SHIFTED), lambda h: (h, 0, 0)),
            pl.BlockSpec((ROWS, 3 * SEG), lambda h: (0, 0)),
        ],
        out_specs=[
            pl.BlockSpec((tokens, HEAD_DIM), lambda h: (0, h)),
            edge_spec,
            mid_spec,
            edge_spec,
            pl.BlockSpec((1, 3, COLS, SHIFTED), lambda h: (h, 0, 0, 0)),
        ],
        out_shape=[
            jax.ShapeDtypeStruct((tokens, width), BF16),
            edge_low,
            jax.ShapeDtypeStruct((2, 3, tokens, width), F32),
            edge_low,
            jax.ShapeDtypeStruct((heads, 3, COLS, SHIFTED), F32),
        ],
        scratch_shapes=[pltpu.VMEM((tokens, 3 * SEG), F32)],
        name="attn_backward",
    )(queries, parts, above, mid, below, bias_rows, mask)


def shift(value, axis, step, wrap):
    count = lax.axis_size(axis)
    pairs = [
        (i, (i + step) % count) for i in range(count) if wrap or 0 <= i + step < count
    ]
    return lax.ppermute(value, axis, pairs)


def make_mask(key_mask):
    lat_total, lon_total = key_mask.shape
    lat, lon = lax.axis_index(LAT), lax.axis_index(LON)
    rows = lax.broadcasted_iota(jnp.int32, key_mask.shape, 0)
    cols = lax.broadcasted_iota(jnp.int32, key_mask.shape, 1)
    valid = ((key_mask == 1) | ((rows % 4 == 0) & (cols % 4 == 0))).astype(F32)
    valid = jnp.pad(valid, ((REACH, SEG_ROWS - ROWS - REACH), (0, 0)))
    valid = jnp.concatenate([valid[:, -COLS:], valid, valid[:, :COLS]], axis=1)
    valid = lax.dynamic_slice(valid, (lat * ROWS, lon * COLS), (SEG_ROWS, 3 * COLS))
    valid = valid.reshape(SEG_ROWS, 3, COLS).transpose(1, 0, 2).reshape(1, 3 * SEG)
    row_of = (lax.broadcasted_iota(jnp.int32, (ROWS, 3 * SEG), 1) // COLS) % SEG_ROWS
    query = lat * ROWS + lax.broadcasted_iota(jnp.int32, (ROWS, 3 * SEG), 0)
    low = jnp.clip(query - REACH, 0, lat_total - WIN) - lat * ROWS + REACH
    allowed = (row_of >= low) & (row_of < low + WIN) & (valid > 0)
    return jnp.where(allowed, 0.0, NEG).astype(F32)


def spread_bias(table):
    heads, offsets, _ = table.shape
    above = ROWS - 1 - REACH
    padded = jnp.pad(
        table,
        ((0, 0), (above, SEG_ROWS + ROWS - offsets - above), (0, 2 * COLS - WIN)),
        constant_values=NEG,
    )
    padded = padded.reshape(heads, SEG_ROWS + ROWS, 2, COLS)
    return padded.transpose(0, 2, 1, 3).reshape(heads, 2, SHIFTED)


def gather_table(spread):
    heads = spread.shape[0]
    offsets = 2 * WIN - 1
    first_row = ROWS - 1 - REACH
    grid = spread.reshape(heads, 3, COLS, SEG_ROWS + ROWS, COLS)[:, :, :, first_row : first_row + offsets]
    pad_y = COLS + 1
    total = jnp.zeros((heads, offsets, WIN + 2 * pad_y), F32)
    for s in range(3):
        for j in range(COLS):
            first = COLS * (s - 1) - j + REACH + pad_y
            total = total + jnp.pad(
                grid[:, s, j], ((0, 0), (0, 0), (first, WIN + 2 * pad_y - COLS - first))
            )
    return total[:, :, pad_y : pad_y + WIN]


def pack_cols(value):
    return value.transpose(0, 2, 1, 3)


def local(queries, keys, values, attn_out, grad_out, w_out, bias_table, key_mask):
    lat_rows, lon_cols, width = queries.shape
    tokens = lat_rows * lon_cols
    feats_local = grad_out.shape[2]
    x_n, chan_n = (lax.axis_size(axis) for axis in ("x", "chan"))
    w_rows_local = w_out.shape[0]
    per_chan = feats_local // (2 * x_n * w_rows_local)
    feats = 2 * w_rows_local
    core, x = lax.axis_index("core"), lax.axis_index("x")
    swap = [(0, 1), (1, 0)]
    skip = COLS - REACH

    grad_t = grad_out.reshape(tokens, feats_local).T
    grad_t = grad_t.reshape(per_chan * 2, x_n, w_rows_local, tokens).transpose(1, 0, 2, 3)
    grad_t = grad_t.reshape(x_n, 1, per_chan * feats, tokens)
    grad_t = jnp.broadcast_to(grad_t, (x_n, chan_n, per_chan * feats, tokens))
    grad_t = grad_t.reshape(x_n * chan_n, per_chan * feats, tokens)
    grad_t, attn_out, w_out, keys, values = lax.optimization_barrier(
        (grad_t, attn_out, w_out, keys, values)
    )
    grad_feats = lax.all_to_all(grad_t, ("x", "chan"), 0, 0)
    grad_feats = grad_feats.reshape(x_n, chan_n, per_chan, feats, tokens)

    w_own = lax.all_gather(w_out, RING, axis=0).reshape(chan_n * feats, width)
    w_other = lax.ppermute(w_own, "core", swap)

    attn_rows = [attn_out.reshape(tokens, width)]
    attn_rows += [shift(attn_rows[0], "x", r, True) for r in range(1, x_n)]

    kv = jnp.stack([keys, values])
    from_left = shift(pack_cols(kv[:, :, skip:]), LON, 1, True)
    from_right = shift(pack_cols(kv[:, :, :REACH]), LON, -1, True)
    left = jnp.pad(pack_cols(from_left), ((0, 0), (0, 0), (skip, 0), (0, 0)))
    right = jnp.pad(pack_cols(from_right), ((0, 0), (0, 0), (0, skip), (0, 0)))
    mid = jnp.stack([left, kv, right], axis=1).reshape(2, 3, tokens, width)
    above = shift(mid[:, :, tokens - EDGE :], LAT, 1, False)
    below = shift(mid[:, :, :EDGE], LAT, -1, False)

    parts = grad_attn_parts(grad_feats, w_own, w_other, core.reshape(1))
    parts, grad_feats = lax.optimization_barrier((parts, grad_feats))
    parts = lax.all_to_all(parts, "x", 0, 0)
    wout_mine, wout_other = grad_wout_parts(grad_feats, attn_rows, jnp.stack([core, x]))
    wout_mine = wout_mine + lax.ppermute(wout_other, "core", swap).astype(F32)
    wout_parts = wout_mine.astype(BF16).reshape(chan_n * 2, w_rows_local, width)
    parts, wout_parts = lax.optimization_barrier((parts, wout_parts))
    wout_parts = lax.all_to_all(wout_parts, RING, 0, 0)
    dq, dabove, dmid, dbelow, spread = attn_backward(
        queries.reshape(tokens, width),
        parts,
        above,
        mid,
        below,
        spread_bias(bias_table),
        make_mask(key_mask),
    )
    from_below = shift(dabove, LAT, -1, False).astype(F32)
    from_above = shift(dbelow, LAT, 1, False).astype(F32)
    table = gather_table(spread)
    table = jnp.pad(table.reshape(-1), (0, -table.size % 128)).reshape(-1, 128)
    gap = tokens - EDGE
    folded = dmid + jnp.pad(from_above, ((0, 0), (0, 0), (0, gap), (0, 0)))
    folded = folded + jnp.pad(from_below, ((0, 0), (0, 0), (gap, 0), (0, 0)))
    folded = folded.reshape(2, 3, lat_rows, lon_cols, width)
    to_left = pack_cols(folded[:, 0, :, skip:].astype(BF16))
    to_right = pack_cols(folded[:, 2, :, :REACH].astype(BF16))
    wout_parts, table = lax.optimization_barrier((wout_parts, table))
    from_right = shift(to_left, LON, -1, True)
    from_left = shift(to_right, LON, 1, True)
    everyone = (*LAT, *LON)
    count = lax.axis_size(everyone)
    table = lax.all_to_all(jnp.broadcast_to(table[None], (count, *table.shape)), everyone, 0, 0)
    grad_table = jnp.sum(table, axis=0).reshape(-1)[: bias_table.size].reshape(bias_table.shape)
    total = folded[:, 1]
    total = total + jnp.pad(
        pack_cols(from_right).astype(F32), ((0, 0), (0, 0), (skip, 0), (0, 0))
    )
    total = total + jnp.pad(
        pack_cols(from_left).astype(F32), ((0, 0), (0, 0), (0, skip), (0, 0))
    )
    total = total.astype(BF16)
    grad_wout = jnp.sum(wout_parts.astype(F32), axis=0)
    return (
        dq.reshape(lat_rows, lon_cols, width),
        total[0],
        total[1],
        grad_wout,
        grad_table,
    )


def solution(mesh):
    lat_n, lon_n, chan_n = (mesh.shape[axis] for axis in ("lat", "lon", "chan"))
    split = jax.sharding.Mesh(
        mesh.devices.reshape(lat_n // 2, 2, 2, lon_n // 2, chan_n), (*LAT, *LON, "chan")
    )
    token_spec = P(LAT, LON, "chan")
    w_spec = P((*LAT, *LON), "chan")
    table_spec = P("chan", None, None)
    return jax.shard_map(
        local,
        mesh=split,
        in_specs=(token_spec,) * 5 + (w_spec, table_spec, P()),
        out_specs=(token_spec,) * 3 + (w_spec, table_spec),
        check_vma=False,
    )
```

time: 230 us -> 157 us (0.68)
  waiting for transfers between devices: 81.5 us -> 27 us
  between operations: 14.3 us -> 1 us
  blocking collectives: 42.3 us -> 29 us
  starting transfers between devices: 46 us -> 55.6 us
  other arithmetic: 4.02 us -> 10.8 us
  Pallas kernels: 24.3 us -> 17.8 us
  local copies, waits for them, and re-layouts: 16.1 us -> 13.6 us
    ppermute x8 -> x11, waiting for transfers between devices: 63 us -> 14.3 us  [shift(): return lax.ppermute(value, axis, pairs)]
    all_to_all x1 -> x0, blocking collectives: 23.1 us -> none  [local(): lax.all_to_all(jnp.broadcast_to(table[None], (lon_n, *table.shape)), 'lon...]
    ppermute x8 -> x11, starting transfers between devices: 20.2 us -> 30.6 us  [shift(): return lax.ppermute(value, axis, pairs)]
    all_gather x1, blocking collectives: 19.2 us -> 29 us  [local(): w_own = lax.all_gather(w_out, RING, axis=0).reshape(chan_n * feats, width)]
    pallas_call x2, Pallas kernels: 17.2 us -> 10.3 us  [the longest x1 5.48 us: grad_wout_parts(): pl.pallas_call(grad_wout_body, grid_spec=pltpu.PrefetchScalarGridSpec(num...]
    all_to_all x4, waiting for transfers between devices: 16.7 us -> 12.8 us  [the longest x1 12.8 us: local(): lax.all_to_all(jnp.broadcast_to(table[None], (count, *table.shape)), ever...]
    convert_element_type x1 -> x2, other arithmetic: 0.06 us -> 3.43 us  [the longest x1 2.19 us: local(): wout_parts = wout_mine.astype(BF16).reshape(chan_n * 2, w_rows_local, width)]
    transpose x0 -> x2, other arithmetic: none -> 2.95 us  [pack_cols(): return value.transpose(0, 2, 1, 3)]
  transfers between devices with their start and end apart: 14 -> 17, of which waited for: 6 -> 5; matrix products, arithmetic and copies ran while one was open for 8% -> 13% of each run, Pallas kernels for 11% -> 11%
where the time goes in v2:
time: 157 us; the launch traced here: 155 us
  starting transfers between devices  55.6 us (35%)
  blocking collectives  29 us (18%)
  waiting for transfers between devices  27 us (17%)
  Pallas kernels  17.8 us (11%)
  local copies, waits for them, and re-layouts  13.6 us (9%)
  other arithmetic  10.8 us (7%)
    ppermute x11, starting transfers between devices, shift(): return lax.ppermute(value, axis, pairs)  30.6 us
    all_gather x1, blocking collectives, local(): w_own = lax.all_gather(w_out, RING, axis=0).reshape(chan_n * feats, width)  29 us
    ppermute x11, waiting for transfers between devices, shift(): return lax.ppermute(value, axis, pairs)  14.3 us
    all_to_all x1, waiting for transfers between devices, local(): lax.all_to_all(jnp.broadcast_to(table[None], (count, *table.shape)), ever...  12.8 us
    all_to_all x1, starting transfers between devices, local(): wout_parts = lax.all_to_all(wout_parts, RING, 0, 0)  8.79 us
    all_to_all x1, starting transfers between devices, local(): lax.all_to_all(jnp.broadcast_to(table[None], (count, *table.shape)), ever...  7.96 us
    pallas_call x1, Pallas kernels, attn_backward(): pl.pallas_call(attn_body, grid=(heads,), in_specs=[pl.BlockSpec((tokens,...  7.45 us
    pallas_call x1, Pallas kernels, grad_wout_parts(): pl.pallas_call(grad_wout_body, grid_spec=pltpu.PrefetchScalarGridSpec(num...  5.48 us
  transfers between devices with their start and end apart: 17, of which 5 were waited for; matrix products, arithmetic and copies ran while one was open for 13% of the time, Pallas kernels for 11%

profile of v2, /device:TPU:32, one launch (start us, length us, event | category | flops | bytes accessed | tf_op | source)
XLA Modules:
  0.0 154.9 jit_solution(14131114968928155850)
XLA Ops:
  3.3 1.6 %collective-permute-start.1 = (bf16[128,640]{1,0:T(8,128)(2,1)S(1)}, bf16[128,640]{1,0:T(8,128)(2,1)}, u32[]{:S(2)}, u32[]{:S(2)}) collective-permute-start(bf16[128,640]{1,0:T(8,128)(2,1)S(1)} %bitcast.177), channel_id=1, source_target_pairs={{0,4},{4,8},{8,12},{12,0},{1,5},{5,9},{9,13},{13,1},{2,6},{6,10},{... | collective-permute-start | bytes 491528 | tf_op jit(solution)/shard_map/ppermute | solution.py:239
  4.8 2.7 %collective-permute-start.2 = (bf16[128,640]{1,0:T(8,128)(2,1)S(1)}, bf16[128,640]{1,0:T(8,128)(2,1)}, u32[]{:S(2)}, u32[]{:S(2)}) collective-permute-start(bf16[128,640]{1,0:T(8,128)(2,1)S(1)} %bitcast.178), channel_id=1, source_target_pairs={{0,8},{4,12},{8,0},{12,4},{1,9},{5,13},{9,1},{13,5},{2,10},{6,14},... | collective-permute-start | bytes 491528 | tf_op jit(solution)/shard_map/ppermute | solution.py:239
  9.0 4.6 %all-to-all-start = ((bf16[16,320,128]{2,1,0:T(8,128)(2,1)}), bf16[16,320,128]{2,1,0:T(8,128)(2,1)S(1)}, u32[]{:S(2)}, u32[]{:S(2)}) async-start(bf16[16,320,128]{2,1,0:T(8,128)(2,1)} %bitcast.7), calls=%async_computation | async-start | bytes 2621440 | tf_op jit(solution)/shard_map/all_to_all | solution.py:311
  13.6 29.0 %all-gather.own_ref = bf16[640,640]{1,0:T(8,128)(2,1)S(1)} all-gather(bf16[80,640]{1,0:T(8,128)(2,1)S(1)} %copy-done.10), channel_id=2, replica_groups=mesh['zl'=4,'core'=2,'zh'=2,'x'=4,'chan'=4] {'zh','zl'}, dimensions={0}, use_global_device_ids=true | all-gather | bytes 921600 | tf_op jit(solution)/shard_map/all_gather | solution.py:314
  43.7 5.0 %collective-permute-start.6 = (bf16[2,6,16,640]{3,1,2,0:T(8,128)(2,1)}, bf16[2,6,16,640]{3,1,2,0:T(8,128)(2,1)}, u32[]{:S(2)}, u32[]{:S(2)}) collective-permute-start(bf16[2,6,16,640]{3,1,2,0:T(8,128)(2,1)} %get-tuple-element.92), channel_id=1, source_target_pairs={{0,28},{4,0},{8,4},{12,8},{16,12},{20,16},{24,20},{28,24},{1,29},{... | collective-permute-start | bytes 737288 | tf_op jit(solution)/shard_map/ppermute | solution.py:239
  51.0 4.8 %grad_attn_parts.1 = bf16[4,128,640]{2,1,0:T(8,128)(2,1)} custom-call(s32[1]{0:T(128)} %bitcast.1.core_ref, bf16[4,4,2,160,128]{4,3,2,1,0:T(8,128)(2,1)} %bitcast.165, bf16[640,640]{1,0:T(8,128)(2,1)} %copy-done.3, bf16[640,640]{1,0:T(8,128)(2,1)} %copy-done.6), custom_call_target="tpu_custom_call" | custom-call | tf_op jit(solution)/shard_map/grad_attn_parts/pallas_call | solution.py:53
  55.9 5.5 %grad_wout_parts.1 = (f32[2,4,80,640]{3,2,1,0:T(8,128)}, bf16[2,4,80,640]{3,2,1,0:T(8,128)(2,1)}) custom-call(s32[2]{0:T(128)} %pad_add_fusion.7.place_ref, bf16[4,4,2,160,128]{4,3,2,1,0:T(8,128)(2,1)} %bitcast.166, bf16[128,640]{1,0:T(8,128)(2,1)} %bitcast.176, bf16[128,640]{1,0:T(8,128)(2,1)} %collective-permute-done.1.refs_1_, ...), custom_call_target="tpu_custom_call" | custom-call | tf_op jit(solution)/shard_map/grad_wout_parts/pallas_call | solution.py:90
  63.6 6.2 %collective-permute-done.5 = bf16[2,6,16,640]{3,1,2,0:T(8,128)(2,1)} collective-permute-done((bf16[2,6,16,640]{3,1,2,0:T(8,128)(2,1)}, bf16[2,6,16,640]{3,1,2,0:T(8,128)(2,1)}, u32[]{:S(2)}, u32[]{:S(2)}) %collective-permute-start.5) | collective-permute-done | bytes 245792 | tf_op jit(solution)/shard_map/ppermute | solution.py:239
  71.1 3.6 %all-to-all-start.1 = ((bf16[4,128,640]{2,1,0:T(8,128)(2,1)}), bf16[4,128,640]{2,1,0:T(8,128)(2,1)S(1)}, u32[]{:S(2)}, u32[]{:S(2)}) async-start(bf16[4,128,640]{2,1,0:T(8,128)(2,1)} %grad_attn_parts.1), calls=%async_computation.1 | async-start | bytes 1310720 | tf_op jit(solution)/shard_map/all_to_all | solution.py:331
  75.6 1.9 %collective-permute-start.7 = (bf16[2,3,48,640]{3,2,1,0:T(8,128)(2,1)}, bf16[2,3,48,640]{3,2,1,0:T(8,128)(2,1)}, u32[]{:S(2)}, u32[]{:S(2)}) collective-permute-start(bf16[2,3,48,640]{3,2,1,0:T(8,128)(2,1)} %get-tuple-element.88), channel_id=1, source_target_pairs={{0,32},{32,64},{64,96},{96,128},{128,160},{160,192},{192,224},{1,3... | collective-permute-start | bytes 1105928 | tf_op jit(solution)/shard_map/ppermute | solution.py:239
  77.6 5.6 %collective-permute-start.8 = (bf16[2,3,48,640]{3,2,1,0:T(8,128)(2,1)}, bf16[2,3,48,640]{3,2,1,0:T(8,128)(2,1)}, u32[]{:S(2)}, u32[]{:S(2)}) collective-permute-start(bf16[2,3,48,640]{3,2,1,0:T(8,128)(2,1)} %get-tuple-element.87), channel_id=1, source_target_pairs={{32,0},{64,32},{96,64},{128,96},{160,128},{192,160},{224,192},{33,... | collective-permute-start | bytes 1105928 | tf_op jit(solution)/shard_map/ppermute | solution.py:239
  83.2 2.2 %add_convert_fusion = bf16[2,4,80,640]{3,2,1,0:T(8,128)(2,1)} fusion(f32[2,4,80,640]{3,2,1,0:T(8,128)S(1)} %copy-done.5, bf16[2,4,80,640]{3,2,1,0:T(8,128)(2,1)} %collective-permute-done.4), kind=kLoop, calls=%fused_computation.2 | loop fusion | flops 1228800 | bytes 3276800 | tf_op jit(solution)/shard_map/convert_element_type | solution.py:334
  85.4 8.8 %all-to-all-start.2 = ((bf16[8,80,640]{2,1,0:T(8,128)(2,1)}), bf16[8,80,640]{2,1,0:T(8,128)(2,1)}, u32[]{:S(2)}, u32[]{:S(2)}) async-start(bf16[8,80,640]{2,1,0:T(8,128)(2,1)} %bitcast.11), calls=%async_computation.2 | async-start | bytes 1638400 | tf_op jit(solution)/shard_map/all_to_all | solution.py:336
  94.9 7.5 %attn_backward.1 = (bf16[128,640]{1,0:T(8,128)(2,1)}, bf16[2,3,48,640]{3,2,1,0:T(8,128)(2,1)}, f32[2,3,128,640]{3,2,1,0:T(8,128)}, bf16[2,3,48,640]{3,2,1,0:T(8,128)(2,1)}, f32[5,3,8,384]{3,2,1,0:T(8,128)}) custom-call(bf16[128,640]{1,0:T(8,128)(2,1)} %bitcast.180, bf16[4,128,640]{2,1,0:T(8,128)(2,1)} %copy-done.4, ...), custom_call_target="tpu_custom_call" | custom-call | tf_op jit(solution)/shard_map/attn_backward/pallas_call | solution.py:203
  102.3 1.9 %collective-permute-start.10 = (bf16[2,3,48,640]{3,2,1,0:T(8,128)(2,1)}, bf16[2,3,48,640]{3,2,1,0:T(8,128)(2,1)S(1)}, u32[]{:S(2)}, u32[]{:S(2)}) collective-permute-start(bf16[2,3,48,640]{3,2,1,0:T(8,128)(2,1)} %get-tuple-element.36), channel_id=1, source_target_pairs={{32,0},{64,32},{96,64},{128,96},{160,128},{192,160},{224,192},{33,... | collective-permute-start | bytes 1105928 | tf_op jit(solution)/shard_map/ppermute | solution.py:239
  104.3 2.4 %collective-permute-start.9 = (bf16[2,3,48,640]{3,2,1,0:T(8,128)(2,1)}, bf16[2,3,48,640]{3,2,1,0:T(8,128)(2,1)}, u32[]{:S(2)}, u32[]{:S(2)}) collective-permute-start(bf16[2,3,48,640]{3,2,1,0:T(8,128)(2,1)} %get-tuple-element.35), channel_id=1, source_target_pairs={{0,32},{32,64},{64,96},{96,128},{128,160},{160,192},{192,224},{1,3... | collective-permute-start | bytes 1105928 | tf_op jit(solution)/shard_map/ppermute | solution.py:239
  106.7 2.5 %reshape.106 = f32[5,3,8,48,8]{4,3,2,1,0:T(8,128)S(1)} reshape(f32[5,3,8,384]{3,2,1,0:T(8,128)} %get-tuple-element.38) | data formatting | bytes 368640 | tf_op jit(solution)/shard_map/reshape | solution.py:275
  110.4 3.7 %collective-permute-done.10 = bf16[2,3,48,640]{3,2,1,0:T(8,128)(2,1)S(1)} collective-permute-done((bf16[2,3,48,640]{3,2,1,0:T(8,128)(2,1)}, bf16[2,3,48,640]{3,2,1,0:T(8,128)(2,1)S(1)}, u32[]{:S(2)}, u32[]{:S(2)}) %collective-permute-start.10) | collective-permute-done | bytes 368672 | tf_op jit(solution)/shard_map/ppermute | solution.py:239
  115.0 1.9 %slice_bitcast_fusion.2 = (bf16[2,6,16,640]{3,1,2,0:T(8,128)(2,1)S(1)}, bf16[2,6,16,640]{3,1,2,0:T(8,128)(2,1)}) fusion(f32[2,3,128,640]{3,2,1,0:T(8,128)S(1)} %copy-done.1, bf16[2,3,48,640]{3,2,1,0:T(8,128)(2,1)S(1)} %collective-permute-done.10, bf16[2,3,48,640]{3,2,1,0:T(8,128)(2,1)} %collective-permute-done.9), kind=kLoop, calls=%fused_computation.9 | loop fusion | flops 1966080 | bytes 3194880 | tf_op jit(solution)/shard_map/transpose | solution.py:288
  117.8 7.1 %collective-permute-start.11 = (bf16[2,6,16,640]{3,1,2,0:T(8,128)(2,1)S(1)}, bf16[2,6,16,640]{3,1,2,0:T(8,128)(2,1)}, u32[]{:S(2)}, u32[]{:S(2)}) collective-permute-start(bf16[2,6,16,640]{3,1,2,0:T(8,128)(2,1)S(1)} %get-tuple-element.85), channel_id=1, source_target_pairs={{0,28},{4,0},{8,4},{12,8},{16,12},{20,16},{24,20},{28,24},{1,29},{... | collective-permute-start | bytes 737288 | tf_op jit(solution)/shard_map/ppermute | solution.py:239
  125.7 8.0 %all-to-all-start.3 = ((f32[64,13,128]{2,1,0:T(8,128)}), f32[64,13,128]{2,1,0:T(8,128)S(1)}, u32[]{:S(2)}, u32[]{:S(2)}) async-start(f32[64,13,128]{2,1,0:T(8,128)} %broadcast_in_dim.25), calls=%async_computation.3 | async-start | bytes 1048576 | tf_op jit(solution)/shard_map/all_to_all | solution.py:361
  133.7 3.4 %collective-permute-done.12 = bf16[2,6,16,640]{3,1,2,0:T(8,128)(2,1)S(1)} collective-permute-done((bf16[2,6,16,640]{3,1,2,0:T(8,128)(2,1)}, bf16[2,6,16,640]{3,1,2,0:T(8,128)(2,1)S(1)}, u32[]{:S(2)}, u32[]{:S(2)}) %collective-permute-start.12) | collective-permute-done | bytes 245792 | tf_op jit(solution)/shard_map/ppermute | solution.py:239
  139.1 1.9 %convert_reduce_fusion = f32[80,640]{1,0:T(8,128)} fusion(bf16[8,80,640]{2,1,0:T(8,128)(2,1)} %all-to-all-done.2), kind=kLoop, calls=%fused_computation.1 | loop fusion | flops 768000 | bytes 1024000 | tf_op jit(solution)/shard_map/reduce_sum | solution.py:371
  141.1 12.8 %all-to-all-done.3 = f32[64,13,128]{2,1,0:T(8,128)S(1)} async-done(((f32[64,13,128]{2,1,0:T(8,128)}), f32[64,13,128]{2,1,0:T(8,128)S(1)}, u32[]{:S(2)}, u32[]{:S(2)}) %all-to-all-start.3) | async-done | bytes 426016 | tf_op jit(solution)/shard_map/all_to_all | solution.py:361
  (82 shorter events, 19.2 us)
Async XLA Ops:
  1.9 11.7 %copy-start.10 = (bf16[80,640]{1,0:T(8,128)(2,1)S(1)}, bf16[80,640]{1,0:T(8,128)(2,1)}, u32[]{:S(2)}) copy-start(bf16[80,640]{1,0:T(8,128)(2,1)} %param.13) | copy-start | bytes 307204
  3.2 39.4 %copy-start.7 = (bf16[16,8,640]{2,1,0:T(8,128)(2,1)S(1)}, bf16[16,8,640]{2,1,0:T(8,128)(2,1)}, u32[]{:S(2)}) copy-start(bf16[16,8,640]{2,1,0:T(8,128)(2,1)} %param.10) | copy-start | bytes 491524
  3.2 39.4 %copy-start.8 = (bf16[16,8,640]{2,1,0:T(8,128)(2,1)S(1)}, bf16[16,8,640]{2,1,0:T(8,128)(2,1)}, u32[]{:S(2)}) copy-start(bf16[16,8,640]{2,1,0:T(8,128)(2,1)} %param.9) | copy-start | bytes 491524
  3.2 45.4 %copy-start.12 = (s32[128,64]{0,1:T(8,128)S(1)}, s32[128,64]{0,1:T(8,128)}, u32[]{:S(2)}) copy-start(s32[128,64]{0,1:T(8,128)} %param.15) | copy-start | bytes 98308
  3.3 45.8 %copy-start.11 = (f32[5,25,13]{1,2,0:T(8,128)S(1)}, f32[5,25,13]{1,2,0:T(8,128)}, u32[]{:S(2)}) copy-start(f32[5,25,13]{1,2,0:T(8,128)} %param.14) | copy-start | bytes 19504
  3.3 52.6 %collective-permute-start.1 = (bf16[128,640]{1,0:T(8,128)(2,1)S(1)}, bf16[128,640]{1,0:T(8,128)(2,1)}, u32[]{:S(2)}, u32[]{:S(2)}) collective-permute-start(bf16[128,640]{1,0:T(8,128)(2,1)S(1)} %bitcast.177), channel_id=1, source_target_pairs={{0,4},{4,8},{8,12},{12,0},{1,5},{5,9},{9,13},{13,1},{2,6},{6,10},{... | collective-permute-start | bytes 491528 | tf_op jit(solution)/shard_map/ppermute | solution.py:239
  4.8 51.0 %collective-permute-start.2 = (bf16[128,640]{1,0:T(8,128)(2,1)S(1)}, bf16[128,640]{1,0:T(8,128)(2,1)}, u32[]{:S(2)}, u32[]{:S(2)}) collective-permute-start(bf16[128,640]{1,0:T(8,128)(2,1)S(1)} %bitcast.178), channel_id=1, source_target_pairs={{0,8},{4,12},{8,0},{12,4},{1,9},{5,13},{9,1},{13,5},{2,10},{6,14},... | collective-permute-start | bytes 491528 | tf_op jit(solution)/shard_map/ppermute | solution.py:239
  7.6 48.3 %collective-permute-start.3 = (bf16[128,640]{1,0:T(8,128)(2,1)S(1)}, bf16[128,640]{1,0:T(8,128)(2,1)}, u32[]{:S(2)}, u32[]{:S(2)}) collective-permute-start(bf16[128,640]{1,0:T(8,128)(2,1)S(1)} %bitcast.179), channel_id=1, source_target_pairs={{0,12},{4,0},{8,4},{12,8},{1,13},{5,1},{9,5},{13,9},{2,14},{6,2},{... | collective-permute-start | bytes 491528 | tf_op jit(solution)/shard_map/ppermute | solution.py:239
  9.0 40.7 %all-to-all-start = ((bf16[16,320,128]{2,1,0:T(8,128)(2,1)}), bf16[16,320,128]{2,1,0:T(8,128)(2,1)S(1)}, u32[]{:S(2)}, u32[]{:S(2)}) async-start(bf16[16,320,128]{2,1,0:T(8,128)(2,1)} %bitcast.7), calls=%async_computation | async-start | bytes 2621440 | tf_op jit(solution)/shard_map/all_to_all | solution.py:311
  42.6 7.1 %collective-permute-start = (bf16[640,640]{1,0:T(8,128)(2,1)S(1)}, bf16[640,640]{1,0:T(8,128)(2,1)S(1)}, u32[]{:S(2)}, u32[]{:S(2)}) collective-permute-start(bf16[640,640]{1,0:T(8,128)(2,1)S(1)} %all-gather.own_ref), channel_id=1, source_target_pairs={{0,32},{32,0},{1,33},{33,1},{2,34},{34,2},{3,35},{35,3},{4,36},{36... | collective-permute-start | bytes 2457608 | tf_op jit(solution)/shard_map/ppermute | solution.py:315
  43.7 18.9 %collective-permute-start.6 = (bf16[2,6,16,640]{3,1,2,0:T(8,128)(2,1)}, bf16[2,6,16,640]{3,1,2,0:T(8,128)(2,1)}, u32[]{:S(2)}, u32[]{:S(2)}) collective-permute-start(bf16[2,6,16,640]{3,1,2,0:T(8,128)(2,1)} %get-tuple-element.92), channel_id=1, source_target_pairs={{0,28},{4,0},{8,4},{12,8},{16,12},{20,16},{24,20},{28,24},{1,29},{... | collective-permute-start | bytes 737288 | tf_op jit(solution)/shard_map/ppermute | solution.py:239
  49.7 20.1 %collective-permute-start.5 = (bf16[2,6,16,640]{3,1,2,0:T(8,128)(2,1)}, bf16[2,6,16,640]{3,1,2,0:T(8,128)(2,1)}, u32[]{:S(2)}, u32[]{:S(2)}) collective-permute-start(bf16[2,6,16,640]{3,1,2,0:T(8,128)(2,1)} %get-tuple-element.91), channel_id=1, source_target_pairs={{0,4},{4,8},{8,12},{12,16},{16,20},{20,24},{24,28},{28,0},{1,5},{5... | collective-permute-start | bytes 737288 | tf_op jit(solution)/shard_map/ppermute | solution.py:239
  61.4 21.8 %collective-permute-start.4 = (bf16[2,4,80,640]{3,2,1,0:T(8,128)(2,1)}, bf16[2,4,80,640]{3,2,1,0:T(8,128)(2,1)}, u32[]{:S(2)}, u32[]{:S(2)}) collective-permute-start(bf16[2,4,80,640]{3,2,1,0:T(8,128)(2,1)} %get-tuple-element.29), channel_id=1, source_target_pairs={{0,32},{32,0},{1,33},{33,1},{2,34},{34,2},{3,35},{35,3},{4,36},{36... | collective-permute-start | bytes 2457608 | tf_op jit(solution)/shard_map/ppermute | solution.py:333
  70.9 12.2 %copy-start.5 = (f32[2,4,80,640]{3,2,1,0:T(8,128)S(1)}, f32[2,4,80,640]{3,2,1,0:T(8,128)}, u32[]{:S(2)}) copy-start(f32[2,4,80,640]{3,2,1,0:T(8,128)} %get-tuple-element.28) | copy-start | bytes 4915204
  71.1 14.3 %copy-start.2 = (bf16[2,3,128,640]{3,2,1,0:T(8,128)(2,1)}, bf16[2,3,128,640]{3,2,1,0:T(8,128)(2,1)S(1)}, u32[]{:S(2)}) copy-start(bf16[2,3,128,640]{3,2,1,0:T(8,128)(2,1)S(1)} %pad_maximum_fusion.mid_ref) | copy-start | bytes 2949124
  71.1 14.3 %all-to-all-start.1 = ((bf16[4,128,640]{2,1,0:T(8,128)(2,1)}), bf16[4,128,640]{2,1,0:T(8,128)(2,1)S(1)}, u32[]{:S(2)}, u32[]{:S(2)}) async-start(bf16[4,128,640]{2,1,0:T(8,128)(2,1)} %grad_attn_parts.1), calls=%async_computation.1 | async-start | bytes 1310720 | tf_op jit(solution)/shard_map/all_to_all | solution.py:331
  75.6 19.2 %collective-permute-start.7 = (bf16[2,3,48,640]{3,2,1,0:T(8,128)(2,1)}, bf16[2,3,48,640]{3,2,1,0:T(8,128)(2,1)}, u32[]{:S(2)}, u32[]{:S(2)}) collective-permute-start(bf16[2,3,48,640]{3,2,1,0:T(8,128)(2,1)} %get-tuple-element.88), channel_id=1, source_target_pairs={{0,32},{32,64},{64,96},{96,128},{128,160},{160,192},{192,224},{1,3... | collective-permute-start | bytes 1105928 | tf_op jit(solution)/shard_map/ppermute | solution.py:239
  77.6 17.3 %collective-permute-start.8 = (bf16[2,3,48,640]{3,2,1,0:T(8,128)(2,1)}, bf16[2,3,48,640]{3,2,1,0:T(8,128)(2,1)}, u32[]{:S(2)}, u32[]{:S(2)}) collective-permute-start(bf16[2,3,48,640]{3,2,1,0:T(8,128)(2,1)} %get-tuple-element.87), channel_id=1, source_target_pairs={{32,0},{64,32},{96,64},{128,96},{160,128},{192,160},{224,192},{33,... | collective-permute-start | bytes 1105928 | tf_op jit(solution)/shard_map/ppermute | solution.py:239
  85.4 39.5 %all-to-all-start.2 = ((bf16[8,80,640]{2,1,0:T(8,128)(2,1)}), bf16[8,80,640]{2,1,0:T(8,128)(2,1)}, u32[]{:S(2)}, u32[]{:S(2)}) async-start(bf16[8,80,640]{2,1,0:T(8,128)(2,1)} %bitcast.11), calls=%async_computation.2 | async-start | bytes 1638400 | tf_op jit(solution)/shard_map/all_to_all | solution.py:336
  102.3 11.8 %collective-permute-start.10 = (bf16[2,3,48,640]{3,2,1,0:T(8,128)(2,1)}, bf16[2,3,48,640]{3,2,1,0:T(8,128)(2,1)S(1)}, u32[]{:S(2)}, u32[]{:S(2)}) collective-permute-start(bf16[2,3,48,640]{3,2,1,0:T(8,128)(2,1)} %get-tuple-element.36), channel_id=1, source_target_pairs={{32,0},{64,32},{96,64},{128,96},{160,128},{192,160},{224,192},{33,... | collective-permute-start | bytes 1105928 | tf_op jit(solution)/shard_map/ppermute | solution.py:239
  104.3 10.7 %collective-permute-start.9 = (bf16[2,3,48,640]{3,2,1,0:T(8,128)(2,1)}, bf16[2,3,48,640]{3,2,1,0:T(8,128)(2,1)}, u32[]{:S(2)}, u32[]{:S(2)}) collective-permute-start(bf16[2,3,48,640]{3,2,1,0:T(8,128)(2,1)} %get-tuple-element.35), channel_id=1, source_target_pairs={{0,32},{32,64},{64,96},{96,128},{128,160},{160,192},{192,224},{1,3... | collective-permute-start | bytes 1105928 | tf_op jit(solution)/shard_map/ppermute | solution.py:239
  116.8 20.3 %collective-permute-start.12 = (bf16[2,6,16,640]{3,1,2,0:T(8,128)(2,1)}, bf16[2,6,16,640]{3,1,2,0:T(8,128)(2,1)S(1)}, u32[]{:S(2)}, u32[]{:S(2)}) collective-permute-start(bf16[2,6,16,640]{3,1,2,0:T(8,128)(2,1)} %get-tuple-element.86), channel_id=1, source_target_pairs={{0,4},{4,8},{8,12},{12,16},{16,20},{20,24},{24,28},{28,0},{1,5},{5... | collective-permute-start | bytes 737288 | tf_op jit(solution)/shard_map/ppermute | solution.py:239
  117.8 19.3 %collective-permute-start.11 = (bf16[2,6,16,640]{3,1,2,0:T(8,128)(2,1)S(1)}, bf16[2,6,16,640]{3,1,2,0:T(8,128)(2,1)}, u32[]{:S(2)}, u32[]{:S(2)}) collective-permute-start(bf16[2,6,16,640]{3,1,2,0:T(8,128)(2,1)S(1)} %get-tuple-element.85), channel_id=1, source_target_pairs={{0,28},{4,0},{8,4},{12,8},{16,12},{20,16},{24,20},{28,24},{1,29},{... | collective-permute-start | bytes 737288 | tf_op jit(solution)/shard_map/ppermute | solution.py:239
  125.7 28.1 %all-to-all-start.3 = ((f32[64,13,128]{2,1,0:T(8,128)}), f32[64,13,128]{2,1,0:T(8,128)S(1)}, u32[]{:S(2)}, u32[]{:S(2)}) async-start(f32[64,13,128]{2,1,0:T(8,128)} %broadcast_in_dim.25), calls=%async_computation.3 | async-start | bytes 1048576 | tf_op jit(solution)/shard_map/all_to_all | solution.py:361
  (6 other events, 26.9 us)

commit v3 on v2

--- a/solution.py
+++ b/solution.py
@@ -4,6 +4,7 @@
 from jax.experimental import pallas as pl
 from jax.experimental.pallas import tpu as pltpu
 from jax.sharding import PartitionSpec as P
+
 
 HEAD_DIM = 128
 WIN = 13
@@ -240,7 +241,7 @@
 
 
 def make_mask(key_mask):
-    lat_total, lon_total = key_mask.shape
+    lat_total, _ = key_mask.shape
     lat, lon = lax.axis_index(LAT), lax.axis_index(LON)
     rows = lax.broadcasted_iota(jnp.int32, key_mask.shape, 0)
     cols = lax.broadcasted_iota(jnp.int32, key_mask.shape, 1)
@@ -311,7 +312,8 @@
     grad_feats = lax.all_to_all(grad_t, ("x", "chan"), 0, 0)
     grad_feats = grad_feats.reshape(x_n, chan_n, per_chan, feats, tokens)
 
-    w_own = lax.all_gather(w_out, RING, axis=0).reshape(chan_n * feats, width)
+    w_own = lax.all_gather(w_out, RING, axis=0)
+    w_own = w_own.reshape(chan_n * feats, width)
     w_other = lax.ppermute(w_own, "core", swap)
 
     attn_rows = [attn_out.reshape(tokens, width)]
@@ -330,7 +332,8 @@
     parts, grad_feats = lax.optimization_barrier((parts, grad_feats))
     parts = lax.all_to_all(parts, "x", 0, 0)
     wout_mine, wout_other = grad_wout_parts(grad_feats, attn_rows, jnp.stack([core, x]))
-    wout_mine = wout_mine + lax.ppermute(wout_other, "core", swap).astype(F32)
+    wout_other = lax.ppermute(wout_other, "core", swap)
+    wout_mine = wout_mine + wout_other.astype(F32)
     wout_parts = wout_mine.astype(BF16).reshape(chan_n * 2, w_rows_local, width)
     parts, wout_parts = lax.optimization_barrier((parts, wout_parts))
     wout_parts = lax.all_to_all(wout_parts, RING, 0, 0)
@@ -358,7 +361,8 @@
     from_left = shift(to_right, LON, 1, True)
     everyone = (*LAT, *LON)
     count = lax.axis_size(everyone)
-    table = lax.all_to_all(jnp.broadcast_to(table[None], (count, *table.shape)), everyone, 0, 0)
+    table = jnp.broadcast_to(table[None], (count, *table.shape))
+    table = lax.all_to_all(table, everyone, 0, 0)
     grad_table = jnp.sum(table, axis=0).reshape(-1)[: bias_table.size].reshape(bias_table.shape)
     total = folded[:, 1]
     total = total + jnp.pad(

time: 157 us -> 157 us (level)
  no operation moved by 1% of the time
where the time goes in v3:
time: 157 us; the launch traced here: 155 us
  starting transfers between devices  55.6 us (35%)
  blocking collectives  29 us (18%)
  waiting for transfers between devices  27 us (17%)
  Pallas kernels  17.8 us (11%)
  local copies, waits for them, and re-layouts  13.6 us (9%)
  other arithmetic  10.8 us (7%)
    ppermute x11, starting transfers between devices, shift(): return lax.ppermute(value, axis, pairs)  30.6 us
    all_gather x1, blocking collectives, local(): w_own = lax.all_gather(w_out, RING, axis=0)  29 us
    ppermute x11, waiting for transfers between devices, shift(): return lax.ppermute(value, axis, pairs)  14.3 us
    all_to_all x1, waiting for transfers between devices, local(): table = lax.all_to_all(table, everyone, 0, 0)  12.8 us
    all_to_all x1, starting transfers between devices, local(): wout_parts = lax.all_to_all(wout_parts, RING, 0, 0)  8.79 us
    all_to_all x1, starting transfers between devices, local(): table = lax.all_to_all(table, everyone, 0, 0)  7.96 us
    pallas_call x1, Pallas kernels, attn_backward(): pl.pallas_call(attn_body, grid=(heads,), in_specs=[pl.BlockSpec((tokens,...  7.45 us
    pallas_call x1, Pallas kernels, grad_wout_parts(): pl.pallas_call(grad_wout_body, grid_spec=pltpu.PrefetchScalarGridSpec(num...  5.48 us
  transfers between devices with their start and end apart: 17, of which 5 were waited for; matrix products, arithmetic and copies ran while one was open for 13% of the time, Pallas kernels for 11%

profile of v3, /device:TPU:32, one launch (start us, length us, event | category | flops | bytes accessed | tf_op | source)
XLA Modules:
  0.0 154.9 jit_solution(14131114968928155850)
XLA Ops:
  3.3 1.6 %collective-permute-start.1 = (bf16[128,640]{1,0:T(8,128)(2,1)S(1)}, bf16[128,640]{1,0:T(8,128)(2,1)}, u32[]{:S(2)}, u32[]{:S(2)}) collective-permute-start(bf16[128,640]{1,0:T(8,128)(2,1)S(1)} %bitcast.177), channel_id=1, source_target_pairs={{0,4},{4,8},{8,12},{12,0},{1,5},{5,9},{9,13},{13,1},{2,6},{6,10},{... | collective-permute-start | bytes 491528 | tf_op jit(solution)/shard_map/ppermute | solution.py:240
  4.8 2.7 %collective-permute-start.2 = (bf16[128,640]{1,0:T(8,128)(2,1)S(1)}, bf16[128,640]{1,0:T(8,128)(2,1)}, u32[]{:S(2)}, u32[]{:S(2)}) collective-permute-start(bf16[128,640]{1,0:T(8,128)(2,1)S(1)} %bitcast.178), channel_id=1, source_target_pairs={{0,8},{4,12},{8,0},{12,4},{1,9},{5,13},{9,1},{13,5},{2,10},{6,14},... | collective-permute-start | bytes 491528 | tf_op jit(solution)/shard_map/ppermute | solution.py:240
  9.0 4.6 %all-to-all-start = ((bf16[16,320,128]{2,1,0:T(8,128)(2,1)}), bf16[16,320,128]{2,1,0:T(8,128)(2,1)S(1)}, u32[]{:S(2)}, u32[]{:S(2)}) async-start(bf16[16,320,128]{2,1,0:T(8,128)(2,1)} %bitcast.7), calls=%async_computation | async-start | bytes 2621440 | tf_op jit(solution)/shard_map/all_to_all | solution.py:312
  13.6 29.0 %all-gather.own_ref = bf16[640,640]{1,0:T(8,128)(2,1)S(1)} all-gather(bf16[80,640]{1,0:T(8,128)(2,1)S(1)} %copy-done.10), channel_id=2, replica_groups=mesh['zl'=4,'core'=2,'zh'=2,'x'=4,'chan'=4] {'zh','zl'}, dimensions={0}, use_global_device_ids=true | all-gather | bytes 921600 | tf_op jit(solution)/shard_map/all_gather | solution.py:315
  43.7 5.0 %collective-permute-start.6 = (bf16[2,6,16,640]{3,1,2,0:T(8,128)(2,1)}, bf16[2,6,16,640]{3,1,2,0:T(8,128)(2,1)}, u32[]{:S(2)}, u32[]{:S(2)}) collective-permute-start(bf16[2,6,16,640]{3,1,2,0:T(8,128)(2,1)} %get-tuple-element.92), channel_id=1, source_target_pairs={{0,28},{4,0},{8,4},{12,8},{16,12},{20,16},{24,20},{28,24},{1,29},{... | collective-permute-start | bytes 737288 | tf_op jit(solution)/shard_map/ppermute | solution.py:240
  51.0 4.8 %grad_attn_parts.1 = bf16[4,128,640]{2,1,0:T(8,128)(2,1)} custom-call(s32[1]{0:T(128)} %bitcast.1.core_ref, bf16[4,4,2,160,128]{4,3,2,1,0:T(8,128)(2,1)} %bitcast.165, bf16[640,640]{1,0:T(8,128)(2,1)} %copy-done.3, bf16[640,640]{1,0:T(8,128)(2,1)} %copy-done.6), custom_call_target="tpu_custom_call" | custom-call | tf_op jit(solution)/shard_map/grad_attn_parts/pallas_call | solution.py:54
  55.9 5.5 %grad_wout_parts.1 = (f32[2,4,80,640]{3,2,1,0:T(8,128)}, bf16[2,4,80,640]{3,2,1,0:T(8,128)(2,1)}) custom-call(s32[2]{0:T(128)} %pad_add_fusion.7.place_ref, bf16[4,4,2,160,128]{4,3,2,1,0:T(8,128)(2,1)} %bitcast.166, bf16[128,640]{1,0:T(8,128)(2,1)} %bitcast.176, bf16[128,640]{1,0:T(8,128)(2,1)} %collective-permute-done.1.refs_1_, ...), custom_call_target="tpu_custom_call" | custom-call | tf_op jit(solution)/shard_map/grad_wout_parts/pallas_call | solution.py:91
  63.6 6.2 %collective-permute-done.5 = bf16[2,6,16,640]{3,1,2,0:T(8,128)(2,1)} collective-permute-done((bf16[2,6,16,640]{3,1,2,0:T(8,128)(2,1)}, bf16[2,6,16,640]{3,1,2,0:T(8,128)(2,1)}, u32[]{:S(2)}, u32[]{:S(2)}) %collective-permute-start.5) | collective-permute-done | bytes 245792 | tf_op jit(solution)/shard_map/ppermute | solution.py:240
  71.1 3.6 %all-to-all-start.1 = ((bf16[4,128,640]{2,1,0:T(8,128)(2,1)}), bf16[4,128,640]{2,1,0:T(8,128)(2,1)S(1)}, u32[]{:S(2)}, u32[]{:S(2)}) async-start(bf16[4,128,640]{2,1,0:T(8,128)(2,1)} %grad_attn_parts.1), calls=%async_computation.1 | async-start | bytes 1310720 | tf_op jit(solution)/shard_map/all_to_all | solution.py:333
  75.6 1.9 %collective-permute-start.7 = (bf16[2,3,48,640]{3,2,1,0:T(8,128)(2,1)}, bf16[2,3,48,640]{3,2,1,0:T(8,128)(2,1)}, u32[]{:S(2)}, u32[]{:S(2)}) collective-permute-start(bf16[2,3,48,640]{3,2,1,0:T(8,128)(2,1)} %get-tuple-element.88), channel_id=1, source_target_pairs={{0,32},{32,64},{64,96},{96,128},{128,160},{160,192},{192,224},{1,3... | collective-permute-start | bytes 1105928 | tf_op jit(solution)/shard_map/ppermute | solution.py:240
  77.6 5.6 %collective-permute-start.8 = (bf16[2,3,48,640]{3,2,1,0:T(8,128)(2,1)}, bf16[2,3,48,640]{3,2,1,0:T(8,128)(2,1)}, u32[]{:S(2)}, u32[]{:S(2)}) collective-permute-start(bf16[2,3,48,640]{3,2,1,0:T(8,128)(2,1)} %get-tuple-element.87), channel_id=1, source_target_pairs={{32,0},{64,32},{96,64},{128,96},{160,128},{192,160},{224,192},{33,... | collective-permute-start | bytes 1105928 | tf_op jit(solution)/shard_map/ppermute | solution.py:240
  83.2 2.2 %add_convert_fusion = bf16[2,4,80,640]{3,2,1,0:T(8,128)(2,1)} fusion(f32[2,4,80,640]{3,2,1,0:T(8,128)S(1)} %copy-done.5, bf16[2,4,80,640]{3,2,1,0:T(8,128)(2,1)} %collective-permute-done.4), kind=kLoop, calls=%fused_computation.2 | loop fusion | flops 1228800 | bytes 3276800 | tf_op jit(solution)/shard_map/convert_element_type | solution.py:337
  85.4 8.8 %all-to-all-start.2 = ((bf16[8,80,640]{2,1,0:T(8,128)(2,1)}), bf16[8,80,640]{2,1,0:T(8,128)(2,1)}, u32[]{:S(2)}, u32[]{:S(2)}) async-start(bf16[8,80,640]{2,1,0:T(8,128)(2,1)} %bitcast.11), calls=%async_computation.2 | async-start | bytes 1638400 | tf_op jit(solution)/shard_map/all_to_all | solution.py:339
  94.9 7.5 %attn_backward.1 = (bf16[128,640]{1,0:T(8,128)(2,1)}, bf16[2,3,48,640]{3,2,1,0:T(8,128)(2,1)}, f32[2,3,128,640]{3,2,1,0:T(8,128)}, bf16[2,3,48,640]{3,2,1,0:T(8,128)(2,1)}, f32[5,3,8,384]{3,2,1,0:T(8,128)}) custom-call(bf16[128,640]{1,0:T(8,128)(2,1)} %bitcast.180, bf16[4,128,640]{2,1,0:T(8,128)(2,1)} %copy-done.4, ...), custom_call_target="tpu_custom_call" | custom-call | tf_op jit(solution)/shard_map/attn_backward/pallas_call | solution.py:204
  102.3 1.9 %collective-permute-start.10 = (bf16[2,3,48,640]{3,2,1,0:T(8,128)(2,1)}, bf16[2,3,48,640]{3,2,1,0:T(8,128)(2,1)S(1)}, u32[]{:S(2)}, u32[]{:S(2)}) collective-permute-start(bf16[2,3,48,640]{3,2,1,0:T(8,128)(2,1)} %get-tuple-element.36), channel_id=1, source_target_pairs={{32,0},{64,32},{96,64},{128,96},{160,128},{192,160},{224,192},{33,... | collective-permute-start | bytes 1105928 | tf_op jit(solution)/shard_map/ppermute | solution.py:240
  104.3 2.4 %collective-permute-start.9 = (bf16[2,3,48,640]{3,2,1,0:T(8,128)(2,1)}, bf16[2,3,48,640]{3,2,1,0:T(8,128)(2,1)}, u32[]{:S(2)}, u32[]{:S(2)}) collective-permute-start(bf16[2,3,48,640]{3,2,1,0:T(8,128)(2,1)} %get-tuple-element.35), channel_id=1, source_target_pairs={{0,32},{32,64},{64,96},{96,128},{128,160},{160,192},{192,224},{1,3... | collective-permute-start | bytes 1105928 | tf_op jit(solution)/shard_map/ppermute | solution.py:240
  106.7 2.5 %reshape.106 = f32[5,3,8,48,8]{4,3,2,1,0:T(8,128)S(1)} reshape(f32[5,3,8,384]{3,2,1,0:T(8,128)} %get-tuple-element.38) | data formatting | bytes 368640 | tf_op jit(solution)/shard_map/reshape | solution.py:276
  110.4 3.7 %collective-permute-done.10 = bf16[2,3,48,640]{3,2,1,0:T(8,128)(2,1)S(1)} collective-permute-done((bf16[2,3,48,640]{3,2,1,0:T(8,128)(2,1)}, bf16[2,3,48,640]{3,2,1,0:T(8,128)(2,1)S(1)}, u32[]{:S(2)}, u32[]{:S(2)}) %collective-permute-start.10) | collective-permute-done | bytes 368672 | tf_op jit(solution)/shard_map/ppermute | solution.py:240
  115.0 1.9 %slice_bitcast_fusion.2 = (bf16[2,6,16,640]{3,1,2,0:T(8,128)(2,1)S(1)}, bf16[2,6,16,640]{3,1,2,0:T(8,128)(2,1)}) fusion(f32[2,3,128,640]{3,2,1,0:T(8,128)S(1)} %copy-done.1, bf16[2,3,48,640]{3,2,1,0:T(8,128)(2,1)S(1)} %collective-permute-done.10, bf16[2,3,48,640]{3,2,1,0:T(8,128)(2,1)} %collective-permute-done.9), kind=kLoop, calls=%fused_computation.9 | loop fusion | flops 1966080 | bytes 3194880 | tf_op jit(solution)/shard_map/transpose | solution.py:289
  117.8 7.1 %collective-permute-start.11 = (bf16[2,6,16,640]{3,1,2,0:T(8,128)(2,1)S(1)}, bf16[2,6,16,640]{3,1,2,0:T(8,128)(2,1)}, u32[]{:S(2)}, u32[]{:S(2)}) collective-permute-start(bf16[2,6,16,640]{3,1,2,0:T(8,128)(2,1)S(1)} %get-tuple-element.85), channel_id=1, source_target_pairs={{0,28},{4,0},{8,4},{12,8},{16,12},{20,16},{24,20},{28,24},{1,29},{... | collective-permute-start | bytes 737288 | tf_op jit(solution)/shard_map/ppermute | solution.py:240
  125.7 8.0 %all-to-all-start.3 = ((f32[64,13,128]{2,1,0:T(8,128)}), f32[64,13,128]{2,1,0:T(8,128)S(1)}, u32[]{:S(2)}, u32[]{:S(2)}) async-start(f32[64,13,128]{2,1,0:T(8,128)} %broadcast_in_dim.25), calls=%async_computation.3 | async-start | bytes 1048576 | tf_op jit(solution)/shard_map/all_to_all | solution.py:365
  133.7 3.4 %collective-permute-done.12 = bf16[2,6,16,640]{3,1,2,0:T(8,128)(2,1)S(1)} collective-permute-done((bf16[2,6,16,640]{3,1,2,0:T(8,128)(2,1)}, bf16[2,6,16,640]{3,1,2,0:T(8,128)(2,1)S(1)}, u32[]{:S(2)}, u32[]{:S(2)}) %collective-permute-start.12) | collective-permute-done | bytes 245792 | tf_op jit(solution)/shard_map/ppermute | solution.py:240
  139.1 1.9 %convert_reduce_fusion = f32[80,640]{1,0:T(8,128)} fusion(bf16[8,80,640]{2,1,0:T(8,128)(2,1)} %all-to-all-done.2), kind=kLoop, calls=%fused_computation.1 | loop fusion | flops 768000 | bytes 1024000 | tf_op jit(solution)/shard_map/reduce_sum | solution.py:375
  141.1 12.8 %all-to-all-done.3 = f32[64,13,128]{2,1,0:T(8,128)S(1)} async-done(((f32[64,13,128]{2,1,0:T(8,128)}), f32[64,13,128]{2,1,0:T(8,128)S(1)}, u32[]{:S(2)}, u32[]{:S(2)}) %all-to-all-start.3) | async-done | bytes 426016 | tf_op jit(solution)/shard_map/all_to_all | solution.py:365
  (82 shorter events, 19.2 us)
Async XLA Ops:
  1.9 11.7 %copy-start.10 = (bf16[80,640]{1,0:T(8,128)(2,1)S(1)}, bf16[80,640]{1,0:T(8,128)(2,1)}, u32[]{:S(2)}) copy-start(bf16[80,640]{1,0:T(8,128)(2,1)} %param.13) | copy-start | bytes 307204
  3.2 39.4 %copy-start.7 = (bf16[16,8,640]{2,1,0:T(8,128)(2,1)S(1)}, bf16[16,8,640]{2,1,0:T(8,128)(2,1)}, u32[]{:S(2)}) copy-start(bf16[16,8,640]{2,1,0:T(8,128)(2,1)} %param.10) | copy-start | bytes 491524
  3.2 39.4 %copy-start.8 = (bf16[16,8,640]{2,1,0:T(8,128)(2,1)S(1)}, bf16[16,8,640]{2,1,0:T(8,128)(2,1)}, u32[]{:S(2)}) copy-start(bf16[16,8,640]{2,1,0:T(8,128)(2,1)} %param.9) | copy-start | bytes 491524
  3.2 45.4 %copy-start.12 = (s32[128,64]{0,1:T(8,128)S(1)}, s32[128,64]{0,1:T(8,128)}, u32[]{:S(2)}) copy-start(s32[128,64]{0,1:T(8,128)} %param.15) | copy-start | bytes 98308
  3.3 45.8 %copy-start.11 = (f32[5,25,13]{1,2,0:T(8,128)S(1)}, f32[5,25,13]{1,2,0:T(8,128)}, u32[]{:S(2)}) copy-start(f32[5,25,13]{1,2,0:T(8,128)} %param.14) | copy-start | bytes 19504
  3.3 52.6 %collective-permute-start.1 = (bf16[128,640]{1,0:T(8,128)(2,1)S(1)}, bf16[128,640]{1,0:T(8,128)(2,1)}, u32[]{:S(2)}, u32[]{:S(2)}) collective-permute-start(bf16[128,640]{1,0:T(8,128)(2,1)S(1)} %bitcast.177), channel_id=1, source_target_pairs={{0,4},{4,8},{8,12},{12,0},{1,5},{5,9},{9,13},{13,1},{2,6},{6,10},{... | collective-permute-start | bytes 491528 | tf_op jit(solution)/shard_map/ppermute | solution.py:240
  4.8 51.0 %collective-permute-start.2 = (bf16[128,640]{1,0:T(8,128)(2,1)S(1)}, bf16[128,640]{1,0:T(8,128)(2,1)}, u32[]{:S(2)}, u32[]{:S(2)}) collective-permute-start(bf16[128,640]{1,0:T(8,128)(2,1)S(1)} %bitcast.178), channel_id=1, source_target_pairs={{0,8},{4,12},{8,0},{12,4},{1,9},{5,13},{9,1},{13,5},{2,10},{6,14},... | collective-permute-start | bytes 491528 | tf_op jit(solution)/shard_map/ppermute | solution.py:240
  7.6 48.3 %collective-permute-start.3 = (bf16[128,640]{1,0:T(8,128)(2,1)S(1)}, bf16[128,640]{1,0:T(8,128)(2,1)}, u32[]{:S(2)}, u32[]{:S(2)}) collective-permute-start(bf16[128,640]{1,0:T(8,128)(2,1)S(1)} %bitcast.179), channel_id=1, source_target_pairs={{0,12},{4,0},{8,4},{12,8},{1,13},{5,1},{9,5},{13,9},{2,14},{6,2},{... | collective-permute-start | bytes 491528 | tf_op jit(solution)/shard_map/ppermute | solution.py:240
  9.0 40.7 %all-to-all-start = ((bf16[16,320,128]{2,1,0:T(8,128)(2,1)}), bf16[16,320,128]{2,1,0:T(8,128)(2,1)S(1)}, u32[]{:S(2)}, u32[]{:S(2)}) async-start(bf16[16,320,128]{2,1,0:T(8,128)(2,1)} %bitcast.7), calls=%async_computation | async-start | bytes 2621440 | tf_op jit(solution)/shard_map/all_to_all | solution.py:312
  42.6 7.1 %collective-permute-start = (bf16[640,640]{1,0:T(8,128)(2,1)S(1)}, bf16[640,640]{1,0:T(8,128)(2,1)S(1)}, u32[]{:S(2)}, u32[]{:S(2)}) collective-permute-start(bf16[640,640]{1,0:T(8,128)(2,1)S(1)} %all-gather.own_ref), channel_id=1, source_target_pairs={{0,32},{32,0},{1,33},{33,1},{2,34},{34,2},{3,35},{35,3},{4,36},{36... | collective-permute-start | bytes 2457608 | tf_op jit(solution)/shard_map/ppermute | solution.py:317
  43.7 18.9 %collective-permute-start.6 = (bf16[2,6,16,640]{3,1,2,0:T(8,128)(2,1)}, bf16[2,6,16,640]{3,1,2,0:T(8,128)(2,1)}, u32[]{:S(2)}, u32[]{:S(2)}) collective-permute-start(bf16[2,6,16,640]{3,1,2,0:T(8,128)(2,1)} %get-tuple-element.92), channel_id=1, source_target_pairs={{0,28},{4,0},{8,4},{12,8},{16,12},{20,16},{24,20},{28,24},{1,29},{... | collective-permute-start | bytes 737288 | tf_op jit(solution)/shard_map/ppermute | solution.py:240
  49.7 20.1 %collective-permute-start.5 = (bf16[2,6,16,640]{3,1,2,0:T(8,128)(2,1)}, bf16[2,6,16,640]{3,1,2,0:T(8,128)(2,1)}, u32[]{:S(2)}, u32[]{:S(2)}) collective-permute-start(bf16[2,6,16,640]{3,1,2,0:T(8,128)(2,1)} %get-tuple-element.91), channel_id=1, source_target_pairs={{0,4},{4,8},{8,12},{12,16},{16,20},{20,24},{24,28},{28,0},{1,5},{5... | collective-permute-start | bytes 737288 | tf_op jit(solution)/shard_map/ppermute | solution.py:240
  61.4 21.8 %collective-permute-start.4 = (bf16[2,4,80,640]{3,2,1,0:T(8,128)(2,1)}, bf16[2,4,80,640]{3,2,1,0:T(8,128)(2,1)}, u32[]{:S(2)}, u32[]{:S(2)}) collective-permute-start(bf16[2,4,80,640]{3,2,1,0:T(8,128)(2,1)} %get-tuple-element.29), channel_id=1, source_target_pairs={{0,32},{32,0},{1,33},{33,1},{2,34},{34,2},{3,35},{35,3},{4,36},{36... | collective-permute-start | bytes 2457608 | tf_op jit(solution)/shard_map/ppermute | solution.py:335
  70.9 12.2 %copy-start.5 = (f32[2,4,80,640]{3,2,1,0:T(8,128)S(1)}, f32[2,4,80,640]{3,2,1,0:T(8,128)}, u32[]{:S(2)}) copy-start(f32[2,4,80,640]{3,2,1,0:T(8,128)} %get-tuple-element.28) | copy-start | bytes 4915204
  71.1 14.3 %copy-start.2 = (bf16[2,3,128,640]{3,2,1,0:T(8,128)(2,1)}, bf16[2,3,128,640]{3,2,1,0:T(8,128)(2,1)S(1)}, u32[]{:S(2)}) copy-start(bf16[2,3,128,640]{3,2,1,0:T(8,128)(2,1)S(1)} %pad_maximum_fusion.mid_ref) | copy-start | bytes 2949124
  71.1 14.3 %all-to-all-start.1 = ((bf16[4,128,640]{2,1,0:T(8,128)(2,1)}), bf16[4,128,640]{2,1,0:T(8,128)(2,1)S(1)}, u32[]{:S(2)}, u32[]{:S(2)}) async-start(bf16[4,128,640]{2,1,0:T(8,128)(2,1)} %grad_attn_parts.1), calls=%async_computation.1 | async-start | bytes 1310720 | tf_op jit(solution)/shard_map/all_to_all | solution.py:333
  75.6 19.2 %collective-permute-start.7 = (bf16[2,3,48,640]{3,2,1,0:T(8,128)(2,1)}, bf16[2,3,48,640]{3,2,1,0:T(8,128)(2,1)}, u32[]{:S(2)}, u32[]{:S(2)}) collective-permute-start(bf16[2,3,48,640]{3,2,1,0:T(8,128)(2,1)} %get-tuple-element.88), channel_id=1, source_target_pairs={{0,32},{32,64},{64,96},{96,128},{128,160},{160,192},{192,224},{1,3... | collective-permute-start | bytes 1105928 | tf_op jit(solution)/shard_map/ppermute | solution.py:240
  77.6 17.3 %collective-permute-start.8 = (bf16[2,3,48,640]{3,2,1,0:T(8,128)(2,1)}, bf16[2,3,48,640]{3,2,1,0:T(8,128)(2,1)}, u32[]{:S(2)}, u32[]{:S(2)}) collective-permute-start(bf16[2,3,48,640]{3,2,1,0:T(8,128)(2,1)} %get-tuple-element.87), channel_id=1, source_target_pairs={{32,0},{64,32},{96,64},{128,96},{160,128},{192,160},{224,192},{33,... | collective-permute-start | bytes 1105928 | tf_op jit(solution)/shard_map/ppermute | solution.py:240
  85.4 39.5 %all-to-all-start.2 = ((bf16[8,80,640]{2,1,0:T(8,128)(2,1)}), bf16[8,80,640]{2,1,0:T(8,128)(2,1)}, u32[]{:S(2)}, u32[]{:S(2)}) async-start(bf16[8,80,640]{2,1,0:T(8,128)(2,1)} %bitcast.11), calls=%async_computation.2 | async-start | bytes 1638400 | tf_op jit(solution)/shard_map/all_to_all | solution.py:339
  102.3 11.8 %collective-permute-start.10 = (bf16[2,3,48,640]{3,2,1,0:T(8,128)(2,1)}, bf16[2,3,48,640]{3,2,1,0:T(8,128)(2,1)S(1)}, u32[]{:S(2)}, u32[]{:S(2)}) collective-permute-start(bf16[2,3,48,640]{3,2,1,0:T(8,128)(2,1)} %get-tuple-element.36), channel_id=1, source_target_pairs={{32,0},{64,32},{96,64},{128,96},{160,128},{192,160},{224,192},{33,... | collective-permute-start | bytes 1105928 | tf_op jit(solution)/shard_map/ppermute | solution.py:240
  104.3 10.7 %collective-permute-start.9 = (bf16[2,3,48,640]{3,2,1,0:T(8,128)(2,1)}, bf16[2,3,48,640]{3,2,1,0:T(8,128)(2,1)}, u32[]{:S(2)}, u32[]{:S(2)}) collective-permute-start(bf16[2,3,48,640]{3,2,1,0:T(8,128)(2,1)} %get-tuple-element.35), channel_id=1, source_target_pairs={{0,32},{32,64},{64,96},{96,128},{128,160},{160,192},{192,224},{1,3... | collective-permute-start | bytes 1105928 | tf_op jit(solution)/shard_map/ppermute | solution.py:240
  116.8 20.3 %collective-permute-start.12 = (bf16[2,6,16,640]{3,1,2,0:T(8,128)(2,1)}, bf16[2,6,16,640]{3,1,2,0:T(8,128)(2,1)S(1)}, u32[]{:S(2)}, u32[]{:S(2)}) collective-permute-start(bf16[2,6,16,640]{3,1,2,0:T(8,128)(2,1)} %get-tuple-element.86), channel_id=1, source_target_pairs={{0,4},{4,8},{8,12},{12,16},{16,20},{20,24},{24,28},{28,0},{1,5},{5... | collective-permute-start | bytes 737288 | tf_op jit(solution)/shard_map/ppermute | solution.py:240
  117.8 19.3 %collective-permute-start.11 = (bf16[2,6,16,640]{3,1,2,0:T(8,128)(2,1)S(1)}, bf16[2,6,16,640]{3,1,2,0:T(8,128)(2,1)}, u32[]{:S(2)}, u32[]{:S(2)}) collective-permute-start(bf16[2,6,16,640]{3,1,2,0:T(8,128)(2,1)S(1)} %get-tuple-element.85), channel_id=1, source_target_pairs={{0,28},{4,0},{8,4},{12,8},{16,12},{20,16},{24,20},{28,24},{1,29},{... | collective-permute-start | bytes 737288 | tf_op jit(solution)/shard_map/ppermute | solution.py:240
  125.7 28.1 %all-to-all-start.3 = ((f32[64,13,128]{2,1,0:T(8,128)}), f32[64,13,128]{2,1,0:T(8,128)S(1)}, u32[]{:S(2)}, u32[]{:S(2)}) async-start(f32[64,13,128]{2,1,0:T(8,128)} %broadcast_in_dim.25), calls=%async_computation.3 | async-start | bytes 1048576 | tf_op jit(solution)/shard_map/all_to_all | solution.py:365
  (6 other events, 26.9 us)
